TPU v7x, 32 devices: a whole 2x2x4 slice. The times are simulated.
32 devices in a mesh: gx: 2 (over y), gy: 4 (over z), gz: 4 (over x, core).
Axes of the slice: x: 2, y: 2, z: 4, core: 2. Of those that a mesh axis runs over, the one named last changes fastest.
Arguments:
- features: bfloat16 [16, 4, 4, 64, 128], P('gx', 'gy', 'gz'), may hold values from -6 to 6
- positions: bfloat16 [16, 4, 4, 3, 128], P('gx', 'gy', 'gz'), may hold values from 0 to 1
- counts: int32 [16, 4, 4], P('gx', 'gy', 'gz'), may hold values from 1 to 128, as said below
- old_cuts: int32 [3], replicated, may hold values from 0 to 8, as said below
- new_cuts: int32 [3], replicated, may hold values from 0 to 8, as said below
- radial_rates: float32 [2, 2], replicated, may hold values from 0.3 to 3
- conv_weight: bfloat16 [2, 64, 2, 64], replicated, may hold values from -0.5 to 0.5
- up_weight: bfloat16 [2, 256, 64], replicated, may hold values from -0.75 to 0.75
- up_bias: float32 [2, 256], replicated, may hold values from -3 to 3
- down_weight: bfloat16 [2, 64, 256], replicated, may hold values from -0.375 to 0.375
- down_bias: float32 [2, 64], replicated, may hold values from -2 to 2
Outputs:
- moved: bfloat16 [16, 4, 4, 64, 128], P('gx', 'gy', 'gz')
Inputs may be any that keep to these rules, and one draw needn't show every extreme that they name: `counts`: some bin of the first x layer holds exactly 128 particles. `old_cuts`: rising from 0 to 8; index k of gx holds the x layers from old_cuts[k] to old_cuts[k+1] - 1, from 2 to 8 of them; with three or more indices along gx one holds exactly 8. `new_cuts`: same form as old_cuts, and each cut differs from the one of old_cuts by -1, 0 or 1.
All inputs are finite; a program needn't handle non-finite values.
Results may differ from a plain program's by a relative error of at most 0.0058.
Values may be sent and summed in bfloat16 or wider, within the bound.
No kernel may reach another device: no remote copies, remote signals or barrier semaphores. Data moves between devices by JAX's collectives and lax.ppermute only.
A program may use at most 128 MiB of HBM per device.

v0:
```python
import functools
import math

import jax
import jax.numpy as jnp
from jax import lax
from jax.experimental import pallas as pl
from jax.experimental.pallas import tpu as pltpu
from jax.sharding import PartitionSpec as P

EPSILON = 1e-05
FAR = float(2**20)
LOG2E = math.log2(math.e)
HEAD = 8


def shift(block, axis, by):
    count = lax.axis_size(axis)
    return lax.ppermute(block, axis, [(i, (i + by) % count) for i in range(count)])


def partner(block, axis):
    count = lax.axis_size(axis)
    return lax.ppermute(block, axis, [(i, i ^ 1) for i in range(count)])


def across(block, axis):
    count = lax.axis_size(axis)
    pairs = [(i, ((i + 1) ^ 1) - 1) for i in range(1, count - 1)]
    return lax.ppermute(block, axis, pairs + [(0, count - 1), (count - 1, 0)])


def split3(value):
    first = value.astype(jnp.bfloat16).astype(jnp.float32)
    rest = value - first
    second = rest.astype(jnp.bfloat16).astype(jnp.float32)
    third = (rest - second).astype(jnp.bfloat16).astype(jnp.float32)
    return first, second, third


def layer_kernel(
    plan,
    ints,
    flts,
    pos_refs,
    feat_refs,
    conv_ref,
    up_ref,
    upb_ref,
    down_ref,
    downb_ref,
    out_ref,
    gath_ref,
):
    frame_rows, feat_rows, out_rows, features, slots = plan
    start, stop = ints[0], ints[1]
    low, high = ints[2], ints[3]
    feat_at, out_at = ints[4], ints[5]
    row8 = lax.broadcasted_iota(jnp.int32, (8, slots), 0)
    row16 = lax.broadcasted_iota(jnp.int32, (8, 2 * slots), 0)
    chan = lax.broadcasted_iota(jnp.int32, (8, 2 * slots), 1) < slots
    rate = jnp.where(chan, flts[0], flts[1]) * LOG2E
    live3 = row16 < 3
    q1, q2, q3 = split3(jnp.where(live3, -rate, 0.0))

    def one_bin(row, carry):
        at = pos_refs[0][0, row, :, :].astype(jnp.float32)
        at = jnp.concatenate([at, at], axis=1)
        square = jnp.sum(jnp.where(live3, at * at, 0.0), axis=0, keepdims=True)
        terms = jnp.where(live3, 2.0 * rate * at, jnp.where(row16 == 4, -rate * square, 0.0))
        a1, a2, a3 = split3(terms)
        first = jnp.where(row16 == 3, -1.0, a1)
        zero = jnp.zeros_like(a1)
        right = jnp.concatenate(
            [first, a2, a3, a1, a2, q1, q2, q3, q1, q2, q1, zero, zero, zero, zero, zero], axis=0
        )
        right = right.T.astype(jnp.bfloat16)
        total = jnp.zeros((features, 2 * slots), jnp.float32)
        for cz in range(3):
            for cy in range(3):
                lefts = []
                feats = []
                for dx in (-1, 0, 1):
                    near = row + dx
                    inside = jnp.logical_and(near >= low, near < high)
                    gone = jnp.where(inside, flts[8 + 3 * cz + cy], FAR)
                    near = jnp.clip(near, 0, frame_rows - 1)
                    move = jnp.where(
                        row8 == 0,
                        float(dx),
                        jnp.where(
                            row8 == 1,
                            flts[2 + cy],
                            jnp.where(
                                row8 == 2, flts[5 + cz], jnp.where(row8 == 3, -gone, jnp.where(row8 == 4, -1.0, 0.0))
                            ),
                        ),
                    )
                    there = pos_refs[cz][cy, near, :, :].astype(jnp.float32) - move
                    b1 = there.astype(jnp.bfloat16).astype(jnp.float32)
                    b2 = there - b1
                    s1, s2, s3 = split3(there * there)
                    empty = jnp.zeros_like(b1)
                    left = jnp.concatenate(
                        [b1, b1, b1, b2, b2, s1, s1, s1, s2, s2, s3, empty, empty, empty, empty, empty],
                        axis=0,
                    ).astype(jnp.bfloat16)
                    lefts.append(left)
                    source = jnp.clip(near - feat_at, 0, feat_rows - 1)
                    feats.append(feat_refs[cz][cy, source, 0:features, :])
                power = jnp.dot(
                    right, jnp.concatenate(lefts, axis=1), preferred_element_type=jnp.float32
                )
                weight = jnp.exp2(power).astype(jnp.bfloat16)
                total = total + lax.dot_general(
                    jnp.concatenate(feats, axis=1),
                    weight,
                    (((1,), (1,)), ((), ())),
                    preferred_element_type=jnp.float32,
                )
        both = jnp.concatenate([total[:, :slots], total[:, slots:]], axis=0)
        gath_ref[row - out_at] = both.astype(jnp.bfloat16)
        return carry

    lax.fori_loop(start, stop, one_bin, 0)

    for place in range(out_ref.shape[0]):
        row = place + out_at
        live = jnp.logical_and(row >= start, row < stop)

        @pl.when(live)
        def _(place=place, row=row):
            mixed = jnp.dot(conv_ref[...], gath_ref[place], preferred_element_type=jnp.float32)
            centred = mixed - jnp.mean(mixed, axis=0, keepdims=True)
            spread = jnp.mean(centred * centred, axis=0, keepdims=True)
            normed = (centred * lax.rsqrt(spread + EPSILON)).astype(jnp.bfloat16)
            hidden = jnp.dot(up_ref[...], normed, preferred_element_type=jnp.float32) + upb_ref[...]
            hidden = jax.nn.silu(hidden).astype(jnp.bfloat16)
            update = (
                jnp.dot(down_ref[...], hidden, preferred_element_type=jnp.float32) + downb_ref[...]
            )
            source = jnp.clip(row - feat_at, 0, feat_rows - 1)
            centre = feat_refs[0][0, source, 0:features, :].astype(jnp.float32)
            held = pos_refs[0][0, row, :, :].astype(jnp.float32)[3:4, :] == 0.0
            result = jnp.where(held, centre + update, 0.0)
            out_ref[place] = result.astype(jnp.bfloat16)

        @pl.when(jnp.logical_not(live))
        def _(place=place):
            out_ref[place] = jnp.zeros(out_ref.shape[1:], out_ref.dtype)


def run_layer(ints, flts, frames, feats, out_rows, conv, up, upb, down, downb):
    frame_rows = frames[0].shape[1]
    feat_rows = feats[0].shape[1]
    features = up.shape[1]
    slots = frames[0].shape[3]
    plan = (frame_rows, feat_rows, out_rows, features, slots)
    same = feats[0] is frames[0]
    channels = conv.shape[1]
    conv2 = conv.reshape(features, channels * features)

    def body(ints, flts, *refs):
        wide = refs[:3]
        where = [ref.at[:, :, features : features + HEAD, :] for ref in wide]
        if same:
            vals, rest = wide, refs[3:]
        else:
            vals, rest = refs[3:6], refs[6:]
        layer_kernel(plan, ints, flts, where, vals, *rest)

    operands = list(frames) + ([] if same else list(feats))
    operands += [conv2, up, upb[:, None], down, downb[:, None]]
    whole = pl.BlockSpec(memory_space=pltpu.VMEM)
    smem = pl.BlockSpec(memory_space=pltpu.SMEM)
    return pl.pallas_call(
        body,
        out_shape=jax.ShapeDtypeStruct((out_rows, features, slots), jnp.bfloat16),
        in_specs=[smem, smem] + [whole] * len(operands),
        out_specs=whole,
        scratch_shapes=[pltpu.VMEM((out_rows, channels * features, slots), jnp.bfloat16)],
        compiler_params=pltpu.CompilerParams(vmem_limit_bytes=48 * 2**20),
    )(ints, flts, *operands)


def local(
    features,
    positions,
    counts,
    old_cuts,
    new_cuts,
    radial_rates,
    conv_weight,
    up_weight,
    up_bias,
    down_weight,
    down_bias,
):
    peers = lax.axis_size("gx")
    column = lax.axis_index("gx")
    row_y = lax.axis_index("gy")
    row_z = lax.axis_index("gz")
    last_y = lax.axis_size("gy") - 1
    last_z = lax.axis_size("gz") - 1
    slot_rows = features.shape[0]
    width = features.shape[3]
    slots = features.shape[4]
    total = peers * slot_rows // 2
    old_low = old_cuts[column]
    old_high = old_cuts[column + 1]
    new_low = new_cuts[column]
    new_high = new_cuts[column + 1]
    held = old_high - old_low

    lane = jnp.arange(slots, dtype=jnp.int32)
    far = jnp.where(lane < counts[..., None], 0.0, FAR).astype(jnp.bfloat16)
    spare = HEAD - positions.shape[3] - 1
    packed = jnp.concatenate(
        [
            features[:, 0, 0],
            positions[:, 0, 0],
            far[:, 0, 0][:, None, :],
            jnp.zeros((slot_rows, spare, slots), jnp.bfloat16),
        ],
        axis=1,
    )

    if peers == 2:
        most = min(slot_rows, total - 2)
        mine = packed[:most]
        other = lax.ppermute(mine, "gx", [(0, 1), (1, 0)])
        frame_rows = total
        base = jnp.int32(0)
        layer = jnp.arange(total, dtype=jnp.int32)
        cut = old_cuts[1]
        owner = (layer >= cut).astype(jnp.int32)
        place = layer - owner * cut
        source = jnp.where(owner == column, place, most + place)
        frame = jnp.take(jnp.concatenate([mine, other], axis=0), source, axis=0)
        mid_rows = total - 1
        mid_at = column
    else:
        reach = 3
        frame_rows = slot_rows + 4
        base = new_low - 2
        pieces = [packed]
        starts = [old_low]
        for by, rows in ((1, reach), (2, 1)):
            tail_at = jnp.maximum(held - rows, 0)
            tail = lax.dynamic_slice_in_dim(packed, tail_at, rows, 0)
            pieces.append(shift(tail, "gx", by))
            back = jnp.maximum(column - by, 0)
            low, high = old_cuts[back], old_cuts[back + 1]
            starts.append(jnp.maximum(low, high - rows))
            pieces.append(shift(packed[:rows], "gx", -by))
            ahead = jnp.minimum(column + by, peers - 1)
            starts.append(old_cuts[ahead])
        layer = base + jnp.arange(frame_rows, dtype=jnp.int32)
        back1 = jnp.maximum(column - 1, 0)
        ahead1 = jnp.minimum(column + 1, peers - 1)
        first = slot_rows
        at = []
        for piece in pieces:
            at.append(first - slot_rows)
            first += piece.shape[0]
        choice = jnp.where(
            layer >= old_high,
            jnp.where(
                layer >= old_cuts[ahead1 + 1], at[4] + layer - starts[4], at[2] + layer - starts[2]
            ),
            jnp.where(
                layer >= old_low,
                layer - old_low,
                jnp.where(
                    layer >= old_cuts[back1], at[1] + layer - starts[1], at[3] + layer - starts[3]
                ),
            ),
        )
        stacked = jnp.concatenate(pieces, axis=0)
        frame = jnp.take(stacked, jnp.clip(choice, 0, stacked.shape[0] - 1), axis=0)
        mid_rows = slot_rows + 2
        mid_at = jnp.int32(1)

    def spread(block):
        trio = jnp.stack([block, shift(block, "gy", 1), shift(block, "gy", -1)])
        return trio, partner(trio, "gz"), across(trio, "gz")

    odd = row_z % 2
    zero = jnp.float32(0.0)
    far_y = [zero, jnp.where(row_y == 0, FAR, 0.0), jnp.where(row_y == last_y, FAR, 0.0)]
    ends = jnp.logical_or(row_z == 0, row_z == last_z)
    far_z = [zero, zero, jnp.where(ends, FAR, 0.0)]
    step_z = jnp.where(odd == 1, -1.0, 1.0)

    def floats(level):
        gone = [jnp.maximum(far_z[cz], far_y[cy]) for cz in range(3) for cy in range(3)]
        return jnp.stack(
            [
                radial_rates[level, 0],
                radial_rates[level, 1],
                zero,
                jnp.float32(-1.0),
                jnp.float32(1.0),
                zero,
                step_z,
                -step_z,
            ]
            + gone
        )

    low = jnp.int32(0) - base
    high = jnp.int32(total) - base
    mid_start = jnp.maximum(new_low - 1, 0) - base
    mid_stop = jnp.minimum(new_high + 1, total) - base
    zero_int = jnp.int32(0)
    frames = spread(frame)
    first_out = run_layer(
        jnp.stack([mid_start, mid_stop, low, high, zero_int, mid_at]),
        floats(0),
        frames,
        frames,
        mid_rows,
        conv_weight[0],
        up_weight[0],
        up_bias[0],
        down_weight[0],
        down_bias[0],
    )
    feats = spread(first_out)
    second = run_layer(
        jnp.stack([new_low - base, new_high - base, low, high, mid_at, new_low - base]),
        floats(1),
        frames,
        feats,
        slot_rows,
        conv_weight[1],
        up_weight[1],
        up_bias[1],
        down_weight[1],
        down_bias[1],
    )
    return second[:, None, None]


def solution(mesh):
    placed = (P("gx", "gy", "gz", None, None),) * 2 + (P("gx", "gy", "gz"),) + (P(),) * 8
    return jax.shard_map(
        local,
        mesh=mesh,
        in_specs=placed,
        out_specs=P("gx", "gy", "gz", None, None),
        check_vma=False,
    )
```

profile of v0, /device:TPU:1, one launch (start us, length us, event | category | flops | bytes accessed | tf_op | source)
XLA Modules:
  0.0 71.4 jit_solution(17534185768905602315)
XLA Ops:
  0.0 0.7 copy-done.8
  0.7 0.1 fusion.1
  0.8 0.1 pad.11.clone
  0.8 1.0 %fusion = bf16[6,72,128]{2,1,0:T(8,128)(2,1)S(1)} fusion(bf16[8,1,128]{2,1,0:T(2,128)(2,1)S(1)} %fusion.1, bf16[8,3,128]{2,1,0:T(4,128)(2,1)S(1)} %copy.18, bf16[8,64,128]{2,1,0:T(8,128)(2,1)} %bitcast.47, bf16[72]{0:T(256)(128)(2,1)S(1)} %pad.11.clone), kind=kLoop, calls=%fused_computation.7 | loop fusion | flops 442368 | bytes 250000 | tf_op jit(solution)/shard_map/concatenate | solution.py:218
  1.9 2.1 %collective-permute-start = (bf16[6,72,128]{2,1,0:T(8,128)(2,1)S(1)}, bf16[6,72,128]{2,1,0:T(8,128)(2,1)S(1)}, u32[]{:S(2)}, u32[]{:S(2)}) collective-permute-start(bf16[6,72,128]{2,1,0:T(8,128)(2,1)S(1)} %fusion), channel_id=1, source_target_pairs={{0,16},{16,0},{1,17},{17,1},{2,18},{18,2},{3,19},{19,3},{4,20},{20... | collective-permute-start | bytes 331784 | tf_op jit(solution)/shard_map/ppermute | solution.py:231
  4.0 0.7 copy-done.9
  4.6 0.7 slice.50
  5.3 0.7 fusion.4
  6.0 0.0 copy-start.1
  6.1 0.8 %copy-done.1 = bf16[2,256,64]{1,2,0:T(8,128)(2,1)S(1)} copy-done((bf16[2,256,64]{1,2,0:T(8,128)(2,1)S(1)}, bf16[2,256,64]{1,2,0:T(8,128)(2,1)}, u32[]{:S(2)}) %copy-start.1) | copy-done | bytes 65560
  6.9 0.7 compare_and_fusion
  7.6 0.0 collective-permute-done
  7.6 0.6 gather_fusion
  8.2 0.1 broadcast_select_fusion
  8.3 3.4 %collective-permute-start.2 = (bf16[8,72,128]{2,1,0:T(8,128)(2,1)S(1)}, bf16[8,72,128]{2,1,0:T(8,128)(2,1)S(1)}, u32[]{:S(2)}, u32[]{:S(2)}) collective-permute-start(bf16[8,72,128]{2,1,0:T(8,128)(2,1)S(1)} %broadcast_select_fusion), channel_id=1, source_target_pairs={{0,12},{4,0},{8,4},{12,8},{1,13},{5,1},{9,5},{13,9},{2,14},{6,2},{... | collective-permute-start | bytes 442376 | tf_op jit(solution)/shard_map/ppermute | solution.py:19
  11.7 0.1 bitcast_select_fusion
  11.8 2.0 %collective-permute-done.2 = bf16[8,72,128]{2,1,0:T(8,128)(2,1)S(1)} collective-permute-done((bf16[8,72,128]{2,1,0:T(8,128)(2,1)S(1)}, bf16[8,72,128]{2,1,0:T(8,128)(2,1)S(1)}, u32[]{:S(2)}, u32[]{:S(2)}) %collective-permute-start.2) | collective-permute-done | bytes 147488 | tf_op jit(solution)/shard_map/ppermute | solution.py:19
  13.8 3.7 %collective-permute-done.1 = bf16[8,72,128]{2,1,0:T(8,128)(2,1)S(1)} collective-permute-done((bf16[8,72,128]{2,1,0:T(8,128)(2,1)S(1)}, bf16[8,72,128]{2,1,0:T(8,128)(2,1)S(1)}, u32[]{:S(2)}, u32[]{:S(2)}) %collective-permute-start.1) | collective-permute-done | bytes 147488 | tf_op jit(solution)/shard_map/ppermute | solution.py:19
  17.5 0.1 pad_maximum_fusion.refs_0_
  17.6 3.5 %collective-permute-start.4 = (bf16[3,8,72,128]{3,2,1,0:T(8,128)(2,1)S(1)}, bf16[3,8,72,128]{3,2,1,0:T(8,128)(2,1)S(1)}, u32[]{:S(2)}, u32[]{:S(2)}) collective-permute-start(bf16[3,8,72,128]{3,2,1,0:T(8,128)(2,1)S(1)} %pad_maximum_fusion.refs_0_), channel_id=1, source_target_pairs={{1,2},{2,1},{0,3},{3,0},{5,6},{6,5},{4,7},{7,4},{9,10},{10,9},{8,1... | collective-permute-start | bytes 1327112 | tf_op jit(solution)/shard_map/ppermute | solution.py:30
  21.1 0.1 copy.21.refs_7_
  21.2 0.1 reshape_squeeze.6.refs_3_
  21.3 0.1 copy.26
  21.4 0.0 copy-start.2
  21.4 0.1 copy.20.refs_5_
  21.6 0.0 copy-start.5
  21.6 0.7 copy-done.5
  22.2 0.6 fusion.8
  24.0 0.0 copy-start.4
  24.0 0.1 stack.85.ints
  24.1 0.6 copy-done.4
  24.7 0.7 fusion.7
  25.4 1.4 %stack.86.flts = f32[17]{0:T(128)S(1)} concatenate(f32[1]{0:T(128)} %bitcast.18, f32[1]{0:T(128)} %bitcast.19, f32[1]{0:T(128)} %constant.61.clone.1, f32[1]{0:T(128)} %constant.62.clone.1, f32[1]{0:T(128)} %constant.63.clone.1, f32[1]{0:T(128)} %constant.61.clone.1, f32[1]{0:T(128)} %bitcast.3, f32[1]{0:T(128)} %bitcast.4, f32[1]{0:T(128)} %constant.61.clone.1, f32[1]{0:T(128)} %bitcast.5, ...), dimensions={0} | concatenate | bytes 136 | tf_op jit(solution)/shard_map/stack | solution.py:297
  26.8 5.2 %collective-permute-done.4.refs_2_ = bf16[3,8,72,128]{3,2,1,0:T(8,128)(2,1)S(1)} collective-permute-done((bf16[3,8,72,128]{3,2,1,0:T(8,128)(2,1)S(1)}, bf16[3,8,72,128]{3,2,1,0:T(8,128)(2,1)S(1)}, u32[]{:S(2)}, u32[]{:S(2)}) %collective-permute-start.4) | collective-permute-done | bytes 442400 | tf_op jit(solution)/shard_map/ppermute | solution.py:30
  32.0 11.6 %shard_map.109 = bf16[7,64,128]{2,1,0:T(8,128)(2,1)S(1)} custom-call(s32[6]{0:T(128)S(1)} %stack.85.ints, f32[17]{0:T(128)S(1)} %stack.86.flts, bf16[3,8,72,128]{3,2,1,0:T(8,128)(2,1)S(1)} %pad_maximum_fusion.refs_0_, bf16[3,8,72,128]{3,2,1,0:T(8,128)(2,1)S(1)} %collective-permute-done.3.refs_1_, bf16[3,8,72,128]{3,2,1,0:T(8,128)(2,1)S(1)} %collective-permute-done.4.refs_2_, ...), custom_call_target="tpu_custom_call" | custom-call | tf_op jit(solution)/shard_map/pallas_call | solution.py:176
  43.6 1.6 %collective-permute-start.6 = (bf16[7,64,128]{2,1,0:T(8,128)(2,1)S(1)}, bf16[7,64,128]{2,1,0:T(8,128)(2,1)S(1)}, u32[]{:S(2)}, u32[]{:S(2)}) collective-permute-start(bf16[7,64,128]{2,1,0:T(8,128)(2,1)S(1)} %shard_map.109), channel_id=1, source_target_pairs={{0,12},{4,0},{8,4},{12,8},{1,13},{5,1},{9,5},{13,9},{2,14},{6,2},{... | collective-permute-start | bytes 344072 | tf_op jit(solution)/shard_map/ppermute | solution.py:19
  45.2 2.8 %collective-permute-done.6 = bf16[7,64,128]{2,1,0:T(8,128)(2,1)S(1)} collective-permute-done((bf16[7,64,128]{2,1,0:T(8,128)(2,1)S(1)}, bf16[7,64,128]{2,1,0:T(8,128)(2,1)S(1)}, u32[]{:S(2)}, u32[]{:S(2)}) %collective-permute-start.6) | collective-permute-done | bytes 114720 | tf_op jit(solution)/shard_map/ppermute | solution.py:19
  48.0 3.1 %collective-permute-done.5 = bf16[7,64,128]{2,1,0:T(8,128)(2,1)S(1)} collective-permute-done((bf16[7,64,128]{2,1,0:T(8,128)(2,1)S(1)}, bf16[7,64,128]{2,1,0:T(8,128)(2,1)S(1)}, u32[]{:S(2)}, u32[]{:S(2)}) %collective-permute-start.5) | collective-permute-done | bytes 114720 | tf_op jit(solution)/shard_map/ppermute | solution.py:19
  51.1 1.6 %collective-permute-start.8 = (bf16[3,7,64,128]{3,2,1,0:T(8,128)(2,1)S(1)}, bf16[3,7,64,128]{3,2,1,0:T(8,128)(2,1)S(1)}, u32[]{:S(2)}, u32[]{:S(2)}) collective-permute-start(bf16[3,7,64,128]{3,2,1,0:T(8,128)(2,1)S(1)} %pad_maximum_fusion.1.refs_3_), channel_id=1, source_target_pairs={{1,2},{2,1},{0,3},{3,0},{5,6},{6,5},{4,7},{7,4},{9,10},{10,9},{8,1... | collective-permute-start | bytes 1032200 | tf_op jit(solution)/shard_map/ppermute | solution.py:30
  52.8 0.0 collective-permute-start.7
  52.8 1.8 %stack.73.ints = s32[6]{0:T(128)S(1)} concatenate(s32[1]{0:T(128)} %get-tuple-element.20, s32[1]{0:T(128)} %get-tuple-element.19, s32[1]{0:T(128)} %constant.59.clone.1, s32[1]{0:T(128)} %constant.60.clone.1, s32[1]{0:T(128)} %bitcast, s32[1]{0:T(128)} %get-tuple-element.20), dimensions={0} | concatenate | bytes 48 | tf_op jit(solution)/shard_map/stack | solution.py:331
  54.6 0.1 copy.24.refs_10_
  54.7 0.1 reshape_squeeze.7.refs_6_
  54.8 0.1 copy.27
  54.9 0.1 copy.23.refs_8_
  55.1 1.3 %stack.81.flts = f32[17]{0:T(128)S(1)} concatenate(f32[1]{0:T(128)} %bitcast.1, f32[1]{0:T(128)} %bitcast.2, f32[1]{0:T(128)} %constant.61.clone.1, f32[1]{0:T(128)} %constant.62.clone.1, f32[1]{0:T(128)} %constant.63.clone.1, f32[1]{0:T(128)} %constant.61.clone.1, f32[1]{0:T(128)} %bitcast.3, f32[1]{0:T(128)} %bitcast.4, f32[1]{0:T(128)} %constant.61.clone.1, f32[1]{0:T(128)} %bitcast.5, ...), dimensions={0} | concatenate | bytes 136 | tf_op jit(solution)/shard_map/stack | solution.py:297
  56.4 4.6 %collective-permute-done.8.refs_5_ = bf16[3,7,64,128]{3,2,1,0:T(8,128)(2,1)S(1)} collective-permute-done((bf16[3,7,64,128]{3,2,1,0:T(8,128)(2,1)S(1)}, bf16[3,7,64,128]{3,2,1,0:T(8,128)(2,1)S(1)}, u32[]{:S(2)}, u32[]{:S(2)}) %collective-permute-start.8) | collective-permute-done | bytes 344096 | tf_op jit(solution)/shard_map/ppermute | solution.py:30
  61.0 10.4 %shard_map.110 = bf16[8,64,128]{2,1,0:T(8,128)(2,1)} custom-call(s32[6]{0:T(128)S(1)} %stack.73.ints, f32[17]{0:T(128)S(1)} %stack.81.flts, bf16[3,8,72,128]{3,2,1,0:T(8,128)(2,1)S(1)} %pad_maximum_fusion.refs_0_, bf16[3,8,72,128]{3,2,1,0:T(8,128)(2,1)S(1)} %collective-permute-done.3.refs_1_, bf16[3,8,72,128]{3,2,1,0:T(8,128)(2,1)S(1)} %collective-permute-done.4.refs_2_, ...), custom_call_target="tpu_custom_call" | custom-call | tf_op jit(solution)/shard_map/pallas_call | solution.py:176
  (26 shorter events, 0.2 us)
Async XLA Ops:
  0.0 0.7 copy-start.8
  0.0 0.7 %copy-start.3 = (bf16[8,1,1,3,128]{4,0,3,2,1:T(8,128)(2,1)S(1)}, bf16[8,1,1,3,128]{4,0,3,2,1:T(8,128)(2,1)}, u32[]{:S(2)}) copy-start(bf16[8,1,1,3,128]{4,0,3,2,1:T(8,128)(2,1)} %param.12) | copy-start | bytes 18436
  0.8 5.2 %copy-start = (bf16[2,64,2,64]{3,2,1,0:T(2,128)(2,1)S(1)}, bf16[2,64,2,64]{3,2,1,0:T(2,128)(2,1)}, u32[]{:S(2)}) copy-start(bf16[2,64,2,64]{3,2,1,0:T(2,128)(2,1)} %param.17) | copy-start | bytes 98308
  1.9 5.7 %collective-permute-start = (bf16[6,72,128]{2,1,0:T(8,128)(2,1)S(1)}, bf16[6,72,128]{2,1,0:T(8,128)(2,1)S(1)}, u32[]{:S(2)}, u32[]{:S(2)}) collective-permute-start(bf16[6,72,128]{2,1,0:T(8,128)(2,1)S(1)} %fusion), channel_id=1, source_target_pairs={{0,16},{16,0},{1,17},{17,1},{2,18},{18,2},{3,19},{19,3},{4,20},{20... | collective-permute-start | bytes 331784 | tf_op jit(solution)/shard_map/ppermute | solution.py:231
  4.0 0.7 copy-start.9
  4.0 1.3 %copy-start.6 = (f32[2,256]{1,0:T(2,128)S(1)}, f32[2,256]{1,0:T(2,128)}, u32[]{:S(2)}) copy-start(f32[2,256]{1,0:T(2,128)} %param.19) | copy-start | bytes 6148
  6.0 0.8 %copy-start.1 = (bf16[2,256,64]{1,2,0:T(8,128)(2,1)S(1)}, bf16[2,256,64]{1,2,0:T(8,128)(2,1)}, u32[]{:S(2)}) copy-start(bf16[2,256,64]{1,2,0:T(8,128)(2,1)} %param.18) | copy-start | bytes 196612
  8.3 5.5 %collective-permute-start.2 = (bf16[8,72,128]{2,1,0:T(8,128)(2,1)S(1)}, bf16[8,72,128]{2,1,0:T(8,128)(2,1)S(1)}, u32[]{:S(2)}, u32[]{:S(2)}) collective-permute-start(bf16[8,72,128]{2,1,0:T(8,128)(2,1)S(1)} %broadcast_select_fusion), channel_id=1, source_target_pairs={{0,12},{4,0},{8,4},{12,8},{1,13},{5,1},{9,5},{13,9},{2,14},{6,2},{... | collective-permute-start | bytes 442376 | tf_op jit(solution)/shard_map/ppermute | solution.py:19
  11.7 5.9 %collective-permute-start.1 = (bf16[8,72,128]{2,1,0:T(8,128)(2,1)S(1)}, bf16[8,72,128]{2,1,0:T(8,128)(2,1)S(1)}, u32[]{:S(2)}, u32[]{:S(2)}) collective-permute-start(bf16[8,72,128]{2,1,0:T(8,128)(2,1)S(1)} %broadcast_select_fusion), channel_id=1, source_target_pairs={{0,4},{4,8},{8,12},{12,0},{1,5},{5,9},{9,13},{13,1},{2,6},{6,10},{... | collective-permute-start | bytes 442376 | tf_op jit(solution)/shard_map/ppermute | solution.py:19
  17.5 3.5 %copy-start.7 = (f32[2,64]{1,0:T(2,128)S(1)}, f32[2,64]{1,0:T(2,128)}, u32[]{:S(2)}) copy-start(f32[2,64]{1,0:T(2,128)} %param.21) | copy-start | bytes 1540
  17.6 14.4 %collective-permute-start.4 = (bf16[3,8,72,128]{3,2,1,0:T(8,128)(2,1)S(1)}, bf16[3,8,72,128]{3,2,1,0:T(8,128)(2,1)S(1)}, u32[]{:S(2)}, u32[]{:S(2)}) collective-permute-start(bf16[3,8,72,128]{3,2,1,0:T(8,128)(2,1)S(1)} %pad_maximum_fusion.refs_0_), channel_id=1, source_target_pairs={{1,2},{2,1},{0,3},{3,0},{5,6},{6,5},{4,7},{7,4},{9,10},{10,9},{8,1... | collective-permute-start | bytes 1327112 | tf_op jit(solution)/shard_map/ppermute | solution.py:30
  21.1 10.9 %collective-permute-start.3 = (bf16[3,8,72,128]{3,2,1,0:T(8,128)(2,1)S(1)}, bf16[3,8,72,128]{3,2,1,0:T(8,128)(2,1)S(1)}, u32[]{:S(2)}, u32[]{:S(2)}) collective-permute-start(bf16[3,8,72,128]{3,2,1,0:T(8,128)(2,1)S(1)} %pad_maximum_fusion.refs_0_), channel_id=1, source_target_pairs={{0,1},{1,0},{2,3},{3,2},{4,5},{5,4},{6,7},{7,6},{8,9},{9,8},{10,11... | collective-permute-start | bytes 1327112 | tf_op jit(solution)/shard_map/ppermute | solution.py:24
  21.4 5.4 %copy-start.2 = (bf16[2,64,256]{2,1,0:T(8,128)(2,1)S(1)}, bf16[2,64,256]{2,1,0:T(8,128)(2,1)}, u32[]{:S(2)}) copy-start(bf16[2,64,256]{2,1,0:T(8,128)(2,1)} %param.20) | copy-start | bytes 196612
  21.6 0.7 copy-start.5
  24.0 0.7 copy-start.4
  43.6 4.4 %collective-permute-start.6 = (bf16[7,64,128]{2,1,0:T(8,128)(2,1)S(1)}, bf16[7,64,128]{2,1,0:T(8,128)(2,1)S(1)}, u32[]{:S(2)}, u32[]{:S(2)}) collective-permute-start(bf16[7,64,128]{2,1,0:T(8,128)(2,1)S(1)} %shard_map.109), channel_id=1, source_target_pairs={{0,12},{4,0},{8,4},{12,8},{1,13},{5,1},{9,5},{13,9},{2,14},{6,2},{... | collective-permute-start | bytes 344072 | tf_op jit(solution)/shard_map/ppermute | solution.py:19
  45.2 5.9 %collective-permute-start.5 = (bf16[7,64,128]{2,1,0:T(8,128)(2,1)S(1)}, bf16[7,64,128]{2,1,0:T(8,128)(2,1)S(1)}, u32[]{:S(2)}, u32[]{:S(2)}) collective-permute-start(bf16[7,64,128]{2,1,0:T(8,128)(2,1)S(1)} %shard_map.109), channel_id=1, source_target_pairs={{0,4},{4,8},{8,12},{12,0},{1,5},{5,9},{9,13},{13,1},{2,6},{6,10},{... | collective-permute-start | bytes 344072 | tf_op jit(solution)/shard_map/ppermute | solution.py:19
  51.1 9.9 %collective-permute-start.8 = (bf16[3,7,64,128]{3,2,1,0:T(8,128)(2,1)S(1)}, bf16[3,7,64,128]{3,2,1,0:T(8,128)(2,1)S(1)}, u32[]{:S(2)}, u32[]{:S(2)}) collective-permute-start(bf16[3,7,64,128]{3,2,1,0:T(8,128)(2,1)S(1)} %pad_maximum_fusion.1.refs_3_), channel_id=1, source_target_pairs={{1,2},{2,1},{0,3},{3,0},{5,6},{6,5},{4,7},{7,4},{9,10},{10,9},{8,1... | collective-permute-start | bytes 1032200 | tf_op jit(solution)/shard_map/ppermute | solution.py:30
  52.8 8.2 %collective-permute-start.7 = (bf16[3,7,64,128]{3,2,1,0:T(8,128)(2,1)S(1)}, bf16[3,7,64,128]{3,2,1,0:T(8,128)(2,1)S(1)}, u32[]{:S(2)}, u32[]{:S(2)}) collective-permute-start(bf16[3,7,64,128]{3,2,1,0:T(8,128)(2,1)S(1)} %pad_maximum_fusion.1.refs_3_), channel_id=1, source_target_pairs={{0,1},{1,0},{2,3},{3,2},{4,5},{5,4},{6,7},{7,6},{8,9},{9,8},{10,11... | collective-permute-start | bytes 1032200 | tf_op jit(solution)/shard_map/ppermute | solution.py:24
where the time goes:
time: 71.9 us; the launch traced here: 71.4 us
  Pallas kernels  22 us (31%)
  waiting for transfers between devices  21.5 us (30%)
  starting transfers between devices  12.2 us (17%)
  local copies, waits for them, and re-layouts  11.5 us (16%)
  other arithmetic  2.76 us (4%)
  between operations  1.43 us (2%)
    pallas_call x2, Pallas kernels, run_layer(): pl.pallas_call(body, out_shape=jax.ShapeDtypeStruct((out_rows, features,...  22 us
    ppermute x4, waiting for transfers between devices, shift(): lax.ppermute(block, axis, [(i, (i + by) % count) for i in range(count)])  11.7 us
    ppermute x2, waiting for transfers between devices, across(): return lax.ppermute(block, axis, pairs + [(0, count - 1), (count - 1, 0)])  9.79 us
    ppermute x2, starting transfers between devices, across(): return lax.ppermute(block, axis, pairs + [(0, count - 1), (count - 1, 0)])  5.13 us
    ppermute x4, starting transfers between devices, shift(): lax.ppermute(block, axis, [(i, (i + by) % count) for i in range(count)])  4.95 us
    unnamed x22, local copies, waits for them, and re-layouts  3.57 us
    another operation x2, local copies, waits for them, and re-layouts, floats(): jnp.stack([radial_rates[level, 0], radial_rates[level, 1], zero, jnp.floa...  2.74 us
    ppermute x1, starting transfers between devices, local(): other = lax.ppermute(mine, 'gx', [(0, 1), (1, 0)])  2.12 us
  transfers between devices with their start and end apart: 9, of which 6 were waited for; matrix products, arithmetic and copies ran while one was open for 13% of the time, Pallas kernels for 0%

commit v1 on v0

v1 whole, which is shorter than its diff:
```python
import functools
import math

import jax
import jax.numpy as jnp
from jax import lax
from jax.experimental import pallas as pl
from jax.experimental.pallas import tpu as pltpu
from jax.sharding import PartitionSpec as P

EPSILON = 1e-05
FAR = float(2**20)
LOG2E = math.log2(math.e)
HEAD = 8


def shift(block, axis, by):
    count = lax.axis_size(axis)
    return lax.ppermute(block, axis, [(i, (i + by) % count) for i in range(count)])


def partner(block, axis):
    count = lax.axis_size(axis)
    return lax.ppermute(block, axis, [(i, i ^ 1) for i in range(count)])


def crossing(block, axis):
    count = lax.axis_size(axis)
    return lax.ppermute(block, axis, [(i, ((i + 1) ^ 1) - 1) for i in range(1, count - 1)])


def split3(value):
    first = value.astype(jnp.bfloat16).astype(jnp.float32)
    rest = value - first
    second = rest.astype(jnp.bfloat16).astype(jnp.float32)
    return first, second, rest - second


def centre_terms(place, row8):
    here = place.astype(jnp.float32)
    live = row8 < 3
    n1, n2, n3 = split3(jnp.sum(jnp.where(live, here * here, 0.0), axis=0, keepdims=True))
    cross = jnp.where(live, -2.0 * here, 0.0)
    ones = jnp.where(live, 1.0, 0.0)
    norm = jnp.where(row8 == 4, n1, jnp.where(row8 == 5, n2, jnp.where(row8 == 6, n3, 0.0)))
    lead = jnp.where(row8 == 3, 1.0, cross + norm)
    stack = jnp.concatenate([lead, cross, cross, ones, ones, ones], axis=0)
    return stack.T.astype(jnp.bfloat16)


def near_terms(place, move):
    there = place.astype(jnp.float32) - move
    pieces = split3(there) + split3(there * there)
    return jnp.concatenate(pieces, axis=0).astype(jnp.bfloat16)


def gather_bins(rows, ints, scales, columns, home, feat_at, row8):
    low, high = ints[2], ints[3]
    sums = []
    for row in rows:
        right = centre_terms(home[row, :, :], row8)
        moves = []
        nears = []
        for dx in (-1, 0, 1):
            near = row + dx
            inside = jnp.logical_and(near >= low, near < high)
            gone = jnp.where(inside, 0.0, FAR)
            moves.append(jnp.where(row8 == 0, float(dx), jnp.where(row8 == 3, -gone, 0.0)))
            nears.append(near)
        items = [(column, dx) for column in columns for dx in range(3)]
        total = None
        for k in range(0, len(items), 2):
            lefts = []
            feats = []
            for (where, vals, base), dx in items[k : k + 2]:
                near = jnp.clip(nears[dx], 0, where.shape[0] - 1)
                lefts.append(near_terms(where[near, :, :], base + moves[dx]))
                source = jnp.clip(near - feat_at, 0, vals.shape[0] - 1)
                feats.append(vals[source, :, :])
            left = lefts[0] if len(lefts) == 1 else jnp.concatenate(lefts, axis=1)
            feat = feats[0] if len(feats) == 1 else jnp.concatenate(feats, axis=1)
            dist = jnp.dot(right, left, preferred_element_type=jnp.float32)
            weight = jnp.concatenate(
                [jnp.exp2(dist * scale).astype(jnp.bfloat16) for scale in scales], axis=0
            )
            part = lax.dot_general(
                feat, weight, (((1,), (1,)), ((), ())), preferred_element_type=jnp.float32
            )
            total = part if total is None else total + part
        sums.append(total)
    return sums


def gather_call(ints, flts, spec, level, home, frames, feats, shape, before, mlp):
    features, slots, head, out_rows, live_rows = shape
    count = len(frames)
    same = feats is None
    channels = 2

    def body(*refs):
        ints, flts = refs[0], refs[1]
        at = 2
        home_ref = refs[at].at[:, features : features + head, :]
        at += 1
        fr = refs[at : at + count]
        at += count
        if same:
            fe = fr
        else:
            fe = refs[at : at + count]
            at += count
        prior = None
        if before is not None:
            prior = refs[at]
            at += 1
        if mlp is not None:
            centre_ref, conv_ref, up_ref, upb_ref, down_ref, downb_ref = refs[at : at + 6]
            at += 6
        out_ref = refs[at]
        row8 = lax.broadcasted_iota(jnp.int32, (head, slots), 0)
        feat_at = ints[4] * (0 if same else 1)
        first = 5 + 2 * level
        start, stop = (ints[0], ints[1]) if level == 0 else (ints[5], ints[6])
        out_at = ints[4] if level == 0 else ints[5]
        scales = [flts[2 * level] * -LOG2E, flts[2 * level + 1] * -LOG2E]
        columns = []
        for index, sub, dy, dz, flags in spec:
            where = fr[index] if sub is None else fr[index].at[sub]
            vals = fe[index] if sub is None else fe[index].at[sub]
            where = where.at[:, features : features + head, :]
            vals = vals.at[:, 0:features, :]
            gone = 0.0
            for flag in flags:
                gone = gone + flts[flag]
            base = jnp.where(row8 == 1, float(dy), 0.0)
            base = jnp.where(row8 == 2, float(dz) * flts[4], base)
            base = jnp.where(row8 == 3, -gone, base)
            base = jnp.where(jnp.logical_and(row8 >= 4, row8 <= 6), -1.0, base)
            columns.append((where, vals, base))

        def step(turn, carry):
            rows = [start + 2 * turn]
            rows.append(jnp.minimum(rows[0] + 1, stop - 1))
            sums = gather_bins(rows, ints, scales, columns, home_ref, feat_at, row8)
            for row, total in zip(rows, sums):
                slot = row - out_at
                if prior is not None:
                    total = total + prior[slot]
                if mlp is None:
                    out_ref[slot] = total
                else:
                    both = jnp.concatenate([total[:, :slots], total[:, slots:]], axis=0)
                    refs[at + 1][slot] = both.astype(jnp.bfloat16)
            return carry

        lax.fori_loop(0, (stop - start + 1) // 2, step, 0)
        if mlp is None:
            return
        gath_ref = refs[at + 1]
        for place in range(0, out_rows, 2):
            group = [p for p in (place, place + 1) if p < live_rows]
            for p in (place, place + 1):
                if p >= live_rows and p < out_rows:
                    out_ref[p] = jnp.zeros((features, slots), jnp.bfloat16)
            if not group:
                continue
            packed = jnp.concatenate([gath_ref[p] for p in group], axis=1)
            mixed = jnp.dot(conv_ref[...], packed, preferred_element_type=jnp.float32)
            centred = mixed - jnp.mean(mixed, axis=0, keepdims=True)
            spread = jnp.mean(centred * centred, axis=0, keepdims=True)
            normed = (centred * lax.rsqrt(spread + EPSILON)).astype(jnp.bfloat16)
            hidden = jnp.dot(up_ref[...], normed, preferred_element_type=jnp.float32)
            hidden = hidden + upb_ref[:, 0 : len(group) * slots]
            half = 0.5 * hidden
            hidden = (half + half * jnp.tanh(half)).astype(jnp.bfloat16)
            update = jnp.dot(down_ref[...], hidden, preferred_element_type=jnp.float32)
            update = update + downb_ref[:, 0 : len(group) * slots]
            for k, p in enumerate(group):
                row = p + out_at
                live = jnp.logical_and(row >= start, row < stop)
                source = jnp.clip(row - feat_at, 0, centre_ref.shape[0] - 1)
                centre = centre_ref[source, 0:features, :].astype(jnp.float32)
                safe = jnp.clip(row, 0, home_ref.shape[0] - 1)
                far = home_ref[safe, :, :].astype(jnp.float32)[3:4, :]
                held = jnp.logical_and(far == 0.0, live)
                result = centre + update[:, k * slots : (k + 1) * slots]
                out_ref[p] = jnp.where(held, result, 0.0).astype(jnp.bfloat16)

    operands = [home] + list(frames) + ([] if same else list(feats))
    if before is not None:
        operands.append(before)
    whole = pl.BlockSpec(memory_space=pltpu.VMEM)
    smem = pl.BlockSpec(memory_space=pltpu.SMEM)
    scratch = []
    if mlp is None:
        out_shape = jax.ShapeDtypeStruct((out_rows, features, channels * slots), jnp.float32)
    else:
        operands += list(mlp)
        out_shape = jax.ShapeDtypeStruct((out_rows, features, slots), jnp.bfloat16)
        scratch = [pltpu.VMEM((out_rows, channels * features, slots), jnp.bfloat16)]
    pairs = live_rows * 3 * len(spec)
    return pl.pallas_call(
        body,
        out_shape=out_shape,
        in_specs=[smem, smem] + [whole] * len(operands),
        out_specs=whole,
        scratch_shapes=scratch,
        cost_estimate=pl.CostEstimate(
            flops=pairs * 2 * slots * slots * (2 * features + 48),
            transcendentals=pairs * 2 * slots * slots,
            bytes_accessed=pairs * 4 * slots * slots,
        ),
        compiler_params=pltpu.CompilerParams(vmem_limit_bytes=32 * 2**20),
    )(ints, flts, *operands)


def local(
    features,
    positions,
    counts,
    old_cuts,
    new_cuts,
    radial_rates,
    conv_weight,
    up_weight,
    up_bias,
    down_weight,
    down_bias,
):
    peers = lax.axis_size("gx")
    column = lax.axis_index("gx")
    row_y = lax.axis_index("gy")
    row_z = lax.axis_index("gz")
    last_y = lax.axis_size("gy") - 1
    last_z = lax.axis_size("gz") - 1
    slot_rows = features.shape[0]
    width = features.shape[3]
    slots = features.shape[4]
    total = peers * slot_rows // 2
    old_low = old_cuts[column]
    old_high = old_cuts[column + 1]
    new_low = new_cuts[column]
    new_high = new_cuts[column + 1]
    held = old_high - old_low

    lane = jnp.arange(slots, dtype=jnp.int32)
    far = jnp.where(lane < counts[..., None], 0.0, FAR).astype(jnp.bfloat16)
    spare = HEAD - positions.shape[3] - 1
    packed = jnp.concatenate(
        [
            features[:, 0, 0],
            positions[:, 0, 0],
            far[:, 0, 0][:, None, :],
            jnp.zeros((slot_rows, spare, slots), jnp.bfloat16),
        ],
        axis=1,
    )

    if peers == 2:
        most = min(slot_rows, total - 2)
        mine = packed[:most]
        other = lax.ppermute(mine, "gx", [(0, 1), (1, 0)])
        frame_rows = total
        base = jnp.int32(0)
        layer = jnp.arange(total, dtype=jnp.int32)
        cut = old_cuts[1]
        owner = (layer >= cut).astype(jnp.int32)
        place = layer - owner * cut
        source = jnp.where(owner == column, place, most + place)
        frame = jnp.take(jnp.concatenate([mine, other], axis=0), source, axis=0)
        mid_rows = total - 1
        mid_at = column
    else:
        reach = 3
        frame_rows = slot_rows + 4
        base = new_low - 2
        pieces = [packed]
        starts = [old_low]
        for by, rows in ((1, reach), (2, 1)):
            tail_at = jnp.maximum(held - rows, 0)
            tail = lax.dynamic_slice_in_dim(packed, tail_at, rows, 0)
            pieces.append(shift(tail, "gx", by))
            back = jnp.maximum(column - by, 0)
            low, high = old_cuts[back], old_cuts[back + 1]
            starts.append(jnp.maximum(low, high - rows))
            pieces.append(shift(packed[:rows], "gx", -by))
            ahead = jnp.minimum(column + by, peers - 1)
            starts.append(old_cuts[ahead])
        layer = base + jnp.arange(frame_rows, dtype=jnp.int32)
        back1 = jnp.maximum(column - 1, 0)
        ahead1 = jnp.minimum(column + 1, peers - 1)
        first = slot_rows
        at = []
        for piece in pieces:
            at.append(first - slot_rows)
            first += piece.shape[0]
        choice = jnp.where(
            layer >= old_high,
            jnp.where(
                layer >= old_cuts[ahead1 + 1], at[4] + layer - starts[4], at[2] + layer - starts[2]
            ),
            jnp.where(
                layer >= old_low,
                layer - old_low,
                jnp.where(
                    layer >= old_cuts[back1], at[1] + layer - starts[1], at[3] + layer - starts[3]
                ),
            ),
        )
        stacked = jnp.concatenate(pieces, axis=0)
        frame = jnp.take(stacked, jnp.clip(choice, 0, stacked.shape[0] - 1), axis=0)
        mid_rows = slot_rows + 2
        mid_at = jnp.int32(1)

    odd = row_z % 2
    ends = jnp.logical_or(row_z == 0, row_z == last_z)
    flts = jnp.concatenate(
        [
            radial_rates.reshape(-1),
            jnp.stack(
                [
                    jnp.where(odd == 1, -1.0, 1.0),
                    jnp.where(row_y == 0, FAR, 0.0),
                    jnp.where(row_y == last_y, FAR, 0.0),
                    jnp.where(ends, FAR, 0.0),
                ]
            ),
        ]
    )
    ints = jnp.stack(
        [
            jnp.maximum(new_low - 1, 0) - base,
            jnp.minimum(new_high + 1, total) - base,
            0 - base,
            total - base,
            mid_at,
            new_low - base,
            new_high - base,
        ]
    )
    up_far, down_far, z_far = 5, 6, 7
    own = [(0, None, 0, 0, ())]
    sides = [
        (0, None, -1, 0, (up_far,)),
        (1, None, 1, 0, (down_far,)),
        (2, 0, 0, 1, ()),
        (2, 1, -1, 1, (up_far,)),
        (2, 2, 1, 1, (down_far,)),
    ]
    cross = [
        (0, 0, 0, -1, (z_far,)),
        (0, 1, -1, -1, (up_far, z_far)),
        (0, 2, 1, -1, (down_far, z_far)),
    ]

    def weights(level):
        conv = conv_weight[level].reshape(width, -1)
        wide = (2 * slots,)
        upb = jnp.broadcast_to(up_bias[level][:, None], up_bias.shape[1:] + wide)
        downb = jnp.broadcast_to(down_bias[level][:, None], down_bias.shape[1:] + wide)
        return (conv, up_weight[level], upb, down_weight[level], downb)

    def layer(level, block, places, out_rows, live_rows):
        shape = (width, slots, HEAD, out_rows, live_rows)
        up = shift(block, "gy", 1)
        down = shift(block, "gy", -1)
        if places is None:
            home, feats1, feats2, feats3 = block, None, None, None
            frames1 = [block]
        else:
            home, up_at, down_at, near_at, far_at = places
            frames1, feats1 = [home], [block]
        first = gather_call(
            ints, flts, own, level, home, frames1, feats1, shape, None, None
        )
        trio = jnp.stack([block, up, down])
        far = crossing(trio, "gz")
        near = partner(trio, "gz")
        if places is None:
            frames2, frames3 = [up, down, near], [far]
        else:
            frames2, feats2 = [up_at, down_at, near_at], [up, down, near]
            frames3, feats3 = [far_at], [far]
        second = gather_call(
            ints, flts, sides, level, home, frames2, feats2, shape, first, None
        )
        out = gather_call(
            ints,
            flts,
            cross,
            level,
            home,
            frames3,
            feats3,
            shape,
            second,
            (block,) + weights(level),
        )
        return out, (block, up, down, near, far)

    mid, places = layer(0, frame, None, mid_rows, mid_rows)
    most = min(slot_rows, total - 2 * (peers - 1))
    second, _ = layer(1, mid, places, slot_rows, most)
    return second[:, None, None]


def solution(mesh):
    placed = (P("gx", "gy", "gz", None, None),) * 2 + (P("gx", "gy", "gz"),) + (P(),) * 8
    return jax.shard_map(
        local,
        mesh=mesh,
        in_specs=placed,
        out_specs=P("gx", "gy", "gz", None, None),
        check_vma=False,
    )
```

time: 71.9 us -> 64.8 us (0.901); the launches traced: 71.4 us -> 65.3 us
  waiting for transfers between devices: 21.5 us -> 9.54 us
  Pallas kernels: 22 us -> 27.1 us
  starting transfers between devices: 12.2 us -> 16.2 us
  local copies, waits for them, and re-layouts: 11.5 us -> 8.3 us
    ppermute x2, waiting for transfers between devices: 9.79 us -> 0.01 us  [crossing(): lax.ppermute(block, axis, [(i, (i + 1 ^ 1) - 1) for i in range(1, count -...]
    pallas_call x2 -> x6, Pallas kernels: 22 us -> 27.1 us  [gather_call(): pl.pallas_call(body, out_shape=out_shape, in_specs=[smem, smem] + [whole]...]
    another operation x12 -> x3, local copies, waits for them, and re-layouts: 5.27 us -> 1.58 us  [the longest x1 1.4 us: local(): jnp.stack([jnp.maximum(new_low - 1, 0) - base, jnp.minimum(new_high + 1,...]
    ppermute x4, waiting for transfers between devices: 11.7 us -> 9.53 us  [shift(): lax.ppermute(block, axis, [(i, (i + by) % count) for i in range(count)])]
    ppermute x4, starting transfers between devices: 4.95 us -> 6.76 us  [shift(): lax.ppermute(block, axis, [(i, (i + by) % count) for i in range(count)])]
    ppermute x2, starting transfers between devices: 0.04 us -> 1.19 us  [partner(): return lax.ppermute(block, axis, [(i, i ^ 1) for i in range(count)])]
    ppermute x2, starting transfers between devices: 5.13 us -> 6.1 us  [crossing(): lax.ppermute(block, axis, [(i, (i + 1 ^ 1) - 1) for i in range(1, count -...]
    unnamed x22 -> x20, local copies, waits for them, and re-layouts: 3.57 us -> 3.49 us
  transfers between devices with their start and end apart: 9 -> 9, of which waited for: 6 -> 4; matrix products, arithmetic and copies ran while one was open for 13% -> 7% of each run, Pallas kernels for 0% -> 24%
where the time goes in v1:
time: 64.8 us; the launch traced here: 65.3 us
  Pallas kernels  27.1 us (42%)
  starting transfers between devices  16.2 us (25%)
  waiting for transfers between devices  9.54 us (15%)
  local copies, waits for them, and re-layouts  8.3 us (13%)
  other arithmetic  2.61 us (4%)
  between operations  1.62 us (2%)
    pallas_call x6, Pallas kernels, gather_call(): pl.pallas_call(body, out_shape=out_shape, in_specs=[smem, smem] + [whole]...  27.1 us
    ppermute x4, waiting for transfers between devices, shift(): lax.ppermute(block, axis, [(i, (i + by) % count) for i in range(count)])  9.53 us
    ppermute x4, starting transfers between devices, shift(): lax.ppermute(block, axis, [(i, (i + by) % count) for i in range(count)])  6.76 us
    ppermute x2, starting transfers between devices, crossing(): lax.ppermute(block, axis, [(i, (i + 1 ^ 1) - 1) for i in range(1, count -...  6.1 us
    unnamed x20, local copies, waits for them, and re-layouts  3.49 us
    ppermute x1, starting transfers between devices, local(): other = lax.ppermute(mine, 'gx', [(0, 1), (1, 0)])  2.12 us
    another operation x1, local copies, waits for them, and re-layouts, local(): jnp.stack([jnp.maximum(new_low - 1, 0) - base, jnp.minimum(new_high + 1,...  1.4 us
  transfers between devices with their start and end apart: 9, of which 4 were waited for; matrix products, arithmetic and copies ran while one was open for 7% of the time, Pallas kernels for 24%

profile of v1, /device:TPU:1, one launch (start us, length us, event | category | flops | bytes accessed | tf_op | source)
XLA Modules:
  0.0 65.3 jit_solution(11919758461025801676)
XLA Ops:
  0.0 0.7 %copy.12 = bf16[8,3,128]{2,1,0:T(4,128)(2,1)S(1)} copy(bf16[8,3,128]{2,0,1:T(8,128)(2,1)} %bitcast.41) | data formatting | bytes 12288 | tf_op jit(solution)/shard_map/squeeze | solution.py:252
  0.7 0.7 copy-done.6
  1.4 0.1 fusion.1
  1.4 0.1 pad.11.clone
  1.5 1.0 %fusion = bf16[6,72,128]{2,1,0:T(8,128)(2,1)S(1)} fusion(bf16[8,1,128]{2,1,0:T(2,128)(2,1)S(1)} %fusion.1, bf16[8,3,128]{2,1,0:T(4,128)(2,1)S(1)} %copy.12, bf16[8,64,128]{2,1,0:T(8,128)(2,1)} %bitcast.40, bf16[72]{0:T(256)(128)(2,1)S(1)} %pad.11.clone), kind=kLoop, calls=%fused_computation.7 | loop fusion | flops 442368 | bytes 250000 | tf_op jit(solution)/shard_map/concatenate | solution.py:249
  2.5 0.0 copy-start
  2.5 2.1 %collective-permute-start = (bf16[6,72,128]{2,1,0:T(8,128)(2,1)S(1)}, bf16[6,72,128]{2,1,0:T(8,128)(2,1)S(1)}, u32[]{:S(2)}, u32[]{:S(2)}) collective-permute-start(bf16[6,72,128]{2,1,0:T(8,128)(2,1)S(1)} %fusion), channel_id=1, source_target_pairs={{0,16},{16,0},{1,17},{17,1},{2,18},{18,2},{3,19},{19,3},{4,20},{20... | collective-permute-start | bytes 331784 | tf_op jit(solution)/shard_map/ppermute | solution.py:262
  4.7 0.1 reshape.118
  4.7 0.7 %copy-done.8 = s32[3]{0:T(128)S(1)} copy-done((s32[3]{0:T(128)S(1)}, s32[3]{0:T(128)}, u32[]{:S(2)}) %copy-start.8) | copy-done | bytes 36
  5.4 0.6 slice.36
  6.0 0.6 fusion.4
  6.7 0.7 %copy-done.4 = f32[2,256]{1,0:T(2,128)S(1)} copy-done((f32[2,256]{1,0:T(2,128)S(1)}, f32[2,256]{1,0:T(2,128)}, u32[]{:S(2)}) %copy-start.4) | copy-done | bytes 2072
  7.4 0.1 copy.16
  7.5 0.7 %copy-done.1 = bf16[2,64,2,64]{3,2,1,0:T(2,128)(2,1)S(1)} copy-done((bf16[2,64,2,64]{3,2,1,0:T(2,128)(2,1)S(1)}, bf16[2,64,2,64]{3,2,1,0:T(2,128)(2,1)}, u32[]{:S(2)}) %copy-start.1) | copy-done | bytes 32792
  8.3 0.1 reshape_squeeze.6.refs_6_
  8.4 0.6 copy-done.3
  8.9 0.7 %fusion.8 = (s32[1]{0:T(128)}, s32[1]{0:T(128)}) fusion(s32[3]{0:T(128)S(1)} %copy-done.3, s32[]{:T(128)S(6)} %select_n.76, s32[]{:T(128)S(6)} %select_n.75), kind=kLoop, calls=%fused_computation.31 | loop fusion | bytes 24 | tf_op jit(solution)/shard_map/dynamic_slice | solution.py:243
  10.9 1.4 %stack.43.refs_0_ = s32[7]{0:T(128)S(1)} concatenate(s32[1]{0:T(128)S(6)} %max.4, s32[1]{0:T(128)S(6)} %min.4, s32[1]{0:T(128)} %constant.55.clone.1, s32[1]{0:T(128)} %constant.59.clone.1, s32[1]{0:T(128)} %bitcast, s32[1]{0:T(128)} %get-tuple-element.16, s32[1]{0:T(128)} %get-tuple-element.15), dimensions={0} | concatenate | bytes 56 | tf_op jit(solution)/shard_map/stack | solution.py:330
  12.3 0.1 concatenate.9.refs_1_
  12.4 0.6 compare_and_fusion
  13.1 0.6 gather_fusion
  13.7 0.1 broadcast_select_fusion.refs_2_.refs_3_.refs_5_
  13.8 1.3 %collective-permute-start.1 = (bf16[8,72,128]{2,1,0:T(8,128)(2,1)S(1)}, bf16[8,72,128]{2,1,0:T(8,128)(2,1)S(1)}, u32[]{:S(2)}, u32[]{:S(2)}) collective-permute-start(bf16[8,72,128]{2,1,0:T(8,128)(2,1)S(1)} %broadcast_select_fusion.refs_2_.refs_3_.refs_5_), channel_id=1, source_target_pairs={{0,4},{4,8},{8,12},{12,0},{1,5},{5,9},{9,13},{13,1},{2,6},{6,10},{... | collective-permute-start | bytes 442376 | tf_op jit(solution)/shard_map/ppermute | solution.py:19
  15.1 2.1 %collective-permute-start.2 = (bf16[8,72,128]{2,1,0:T(8,128)(2,1)S(1)}, bf16[8,72,128]{2,1,0:T(8,128)(2,1)S(1)}, u32[]{:S(2)}, u32[]{:S(2)}) collective-permute-start(bf16[8,72,128]{2,1,0:T(8,128)(2,1)S(1)} %broadcast_select_fusion.refs_2_.refs_3_.refs_5_), channel_id=1, source_target_pairs={{0,12},{4,0},{8,4},{12,8},{1,13},{5,1},{9,5},{13,9},{2,14},{6,2},{... | collective-permute-start | bytes 442376 | tf_op jit(solution)/shard_map/ppermute | solution.py:19
  17.2 0.1 bitcast_select_fusion
  17.3 2.9 %collective-permute-done.1.refs_3_ = bf16[8,72,128]{2,1,0:T(8,128)(2,1)S(1)} collective-permute-done((bf16[8,72,128]{2,1,0:T(8,128)(2,1)S(1)}, bf16[8,72,128]{2,1,0:T(8,128)(2,1)S(1)}, u32[]{:S(2)}, u32[]{:S(2)}) %collective-permute-start.1) | collective-permute-done | bytes 147488 | tf_op jit(solution)/shard_map/ppermute | solution.py:19
  20.2 3.3 %collective-permute-done.2.refs_4_ = bf16[8,72,128]{2,1,0:T(8,128)(2,1)S(1)} collective-permute-done((bf16[8,72,128]{2,1,0:T(8,128)(2,1)S(1)}, bf16[8,72,128]{2,1,0:T(8,128)(2,1)S(1)}, u32[]{:S(2)}, u32[]{:S(2)}) %collective-permute-start.2) | collective-permute-done | bytes 147488 | tf_op jit(solution)/shard_map/ppermute | solution.py:19
  23.5 0.1 pad_maximum_fusion
  23.5 1.1 %collective-permute-start.4 = (bf16[3,8,72,128]{3,2,1,0:T(8,128)(2,1)S(1)}, bf16[3,8,72,128]{3,2,1,0:T(8,128)(2,1)S(1)}, u32[]{:S(2)}, u32[]{:S(2)}) collective-permute-start(bf16[3,8,72,128]{3,2,1,0:T(8,128)(2,1)S(1)} %pad_maximum_fusion), channel_id=1, source_target_pairs={{0,1},{1,0},{2,3},{3,2},{4,5},{5,4},{6,7},{7,6},{8,9},{9,8},{10,11... | collective-permute-start | bytes 1327112 | tf_op jit(solution)/shard_map/ppermute | solution.py:24
  24.7 3.0 %collective-permute-start.3 = (bf16[3,8,72,128]{3,2,1,0:T(8,128)(2,1)S(1)}, bf16[3,8,72,128]{3,2,1,0:T(8,128)(2,1)S(1)}, u32[]{:S(2)}, u32[]{:S(2)}) collective-permute-start(bf16[3,8,72,128]{3,2,1,0:T(8,128)(2,1)S(1)} %pad_maximum_fusion), channel_id=1, source_target_pairs={{1,2},{2,1},{5,6},{6,5},{9,10},{10,9},{13,14},{14,13},{17,18},{18,... | collective-permute-start | bytes 1327112 | tf_op jit(solution)/shard_map/ppermute | solution.py:29
  27.7 2.7 %shard_map.109.refs_6_ = f32[7,64,256]{2,1,0:T(8,128)S(1)} custom-call(s32[7]{0:T(128)S(1)} %stack.43.refs_0_, f32[8]{0:T(128)S(1)} %concatenate.9.refs_1_, bf16[8,72,128]{2,1,0:T(8,128)(2,1)S(1)} %broadcast_select_fusion.refs_2_.refs_3_.refs_5_, bf16[8,72,128]{2,1,0:T(8,128)(2,1)S(1)} %broadcast_select_fusion.refs_2_.refs_3_.refs_5_), custom_call_target="tpu_custom_call" | custom-call | flops 121110528 | bytes 1376256 | tf_op jit(solution)/shard_map/pallas_call | solution.py:202
  30.5 5.2 %shard_map.110.refs_4_ = f32[7,64,256]{2,1,0:T(8,128)S(1)} custom-call(s32[7]{0:T(128)S(1)} %stack.43.refs_0_, f32[8]{0:T(128)S(1)} %concatenate.9.refs_1_, bf16[8,72,128]{2,1,0:T(8,128)(2,1)S(1)} %broadcast_select_fusion.refs_2_.refs_3_.refs_5_, bf16[8,72,128]{2,1,0:T(8,128)(2,1)S(1)} %collective-permute-done.1.refs_3_, ...), custom_call_target="tpu_custom_call" | custom-call | flops 605552640 | bytes 6881280 | tf_op jit(solution)/shard_map/pallas_call | solution.py:202
  35.7 0.1 broadcast_in_dim.66.refs_8_
  35.8 0.1 broadcast_in_dim.68.refs_10_
  35.9 5.6 %shard_map.111.refs_4_.refs_6_ = bf16[7,64,128]{2,1,0:T(8,128)(2,1)S(1)} custom-call(s32[7]{0:T(128)S(1)} %stack.43.refs_0_, f32[8]{0:T(128)S(1)} %concatenate.9.refs_1_, bf16[8,72,128]{2,1,0:T(8,128)(2,1)S(1)} %broadcast_select_fusion.refs_2_.refs_3_.refs_5_, bf16[3,8,72,128]{3,2,1,0:T(8,128)(2,1)S(1)} %collective-permute-done.3.refs_3_, ...), custom_call_target="tpu_custom_call" | custom-call | flops 363331584 | bytes 4128768 | tf_op jit(solution)/shard_map/pallas_call | solution.py:202
  41.4 0.9 %collective-permute-start.5 = (bf16[7,64,128]{2,1,0:T(8,128)(2,1)S(1)}, bf16[7,64,128]{2,1,0:T(8,128)(2,1)S(1)}, u32[]{:S(2)}, u32[]{:S(2)}) collective-permute-start(bf16[7,64,128]{2,1,0:T(8,128)(2,1)S(1)} %shard_map.111.refs_4_.refs_6_), channel_id=1, source_target_pairs={{0,4},{4,8},{8,12},{12,0},{1,5},{5,9},{9,13},{13,1},{2,6},{6,10},{... | collective-permute-start | bytes 344072 | tf_op jit(solution)/shard_map/ppermute | solution.py:19
  42.3 2.4 %collective-permute-start.6 = (bf16[7,64,128]{2,1,0:T(8,128)(2,1)S(1)}, bf16[7,64,128]{2,1,0:T(8,128)(2,1)S(1)}, u32[]{:S(2)}, u32[]{:S(2)}) collective-permute-start(bf16[7,64,128]{2,1,0:T(8,128)(2,1)S(1)} %shard_map.111.refs_4_.refs_6_), channel_id=1, source_target_pairs={{0,12},{4,0},{8,4},{12,8},{1,13},{5,1},{9,5},{13,9},{2,14},{6,2},{... | collective-permute-start | bytes 344072 | tf_op jit(solution)/shard_map/ppermute | solution.py:19
  44.7 2.9 %collective-permute-done.5.refs_6_ = bf16[7,64,128]{2,1,0:T(8,128)(2,1)S(1)} collective-permute-done((bf16[7,64,128]{2,1,0:T(8,128)(2,1)S(1)}, bf16[7,64,128]{2,1,0:T(8,128)(2,1)S(1)}, u32[]{:S(2)}, u32[]{:S(2)}) %collective-permute-start.5) | collective-permute-done | bytes 114720 | tf_op jit(solution)/shard_map/ppermute | solution.py:19
  47.7 0.4 collective-permute-done.6.refs_7_
  48.1 0.1 collective-permute-start.8
  48.2 3.1 %collective-permute-start.7 = (bf16[3,7,64,128]{3,2,1,0:T(8,128)(2,1)S(1)}, bf16[3,7,64,128]{3,2,1,0:T(8,128)(2,1)S(1)}, u32[]{:S(2)}, u32[]{:S(2)}) collective-permute-start(bf16[3,7,64,128]{3,2,1,0:T(8,128)(2,1)S(1)} %pad_maximum_fusion.1), channel_id=1, source_target_pairs={{1,2},{2,1},{5,6},{6,5},{9,10},{10,9},{13,14},{14,13},{17,18},{18,... | collective-permute-start | bytes 1032200 | tf_op jit(solution)/shard_map/ppermute | solution.py:29
  51.3 0.1 copy.17
  51.4 0.1 reshape_squeeze.7.refs_7_
  51.5 2.7 %shard_map.112.refs_9_ = f32[8,64,256]{2,1,0:T(8,128)S(1)} custom-call(s32[7]{0:T(128)S(1)} %stack.43.refs_0_, f32[8]{0:T(128)S(1)} %concatenate.9.refs_1_, bf16[8,72,128]{2,1,0:T(8,128)(2,1)S(1)} %broadcast_select_fusion.refs_2_.refs_3_.refs_5_, bf16[8,72,128]{2,1,0:T(8,128)(2,1)S(1)} %broadcast_select_fusion.refs_2_.refs_3_.refs_5_, ...), custom_call_target="tpu_custom_call" | custom-call | flops 103809024 | bytes 1179648 | tf_op jit(solution)/shard_map/pallas_call | solution.py:202
  54.3 5.2 %shard_map.113.refs_5_ = f32[8,64,256]{2,1,0:T(8,128)S(1)} custom-call(s32[7]{0:T(128)S(1)} %stack.43.refs_0_, f32[8]{0:T(128)S(1)} %concatenate.9.refs_1_, bf16[8,72,128]{2,1,0:T(8,128)(2,1)S(1)} %broadcast_select_fusion.refs_2_.refs_3_.refs_5_, bf16[8,72,128]{2,1,0:T(8,128)(2,1)S(1)} %collective-permute-done.1.refs_3_, ...), custom_call_target="tpu_custom_call" | custom-call | flops 519045120 | bytes 5898240 | tf_op jit(solution)/shard_map/pallas_call | solution.py:202
  59.4 0.1 broadcast_in_dim.70.refs_9_
  59.6 0.1 broadcast_in_dim.72.refs_11_
  59.6 5.7 %shard_map.114 = bf16[8,64,128]{2,1,0:T(8,128)(2,1)} custom-call(s32[7]{0:T(128)S(1)} %stack.43.refs_0_, f32[8]{0:T(128)S(1)} %concatenate.9.refs_1_, bf16[8,72,128]{2,1,0:T(8,128)(2,1)S(1)} %broadcast_select_fusion.refs_2_.refs_3_.refs_5_, bf16[3,8,72,128]{3,2,1,0:T(8,128)(2,1)S(1)} %collective-permute-done.3.refs_3_, ...), custom_call_target="tpu_custom_call" | custom-call | flops 311427072 | bytes 3538944 | tf_op jit(solution)/shard_map/pallas_call | solution.py:202
  (26 shorter events, 0.2 us)
Async XLA Ops:
  0.7 0.7 %copy-start.6 = (s32[8,1,1]{0,2,1:T(1,128)S(1)}, s32[8,1,1]{0,2,1:T(1,128)}, u32[]{:S(2)}) copy-start(s32[8,1,1]{0,2,1:T(1,128)} %param.13) | copy-start | bytes 100
  1.5 3.1 %copy-start.7 = (f32[2,2]{1,0:T(2,128)S(1)}, f32[2,2]{1,0:T(2,128)}, u32[]{:S(2)}) copy-start(f32[2,2]{1,0:T(2,128)} %param.16) | copy-start | bytes 52
  2.5 4.8 %copy-start = (bf16[2,256,64]{1,2,0:T(8,128)(2,1)S(1)}, bf16[2,256,64]{1,2,0:T(8,128)(2,1)}, u32[]{:S(2)}) copy-start(bf16[2,256,64]{1,2,0:T(8,128)(2,1)} %param.18) | copy-start | bytes 196612
  2.5 10.5 %collective-permute-start = (bf16[6,72,128]{2,1,0:T(8,128)(2,1)S(1)}, bf16[6,72,128]{2,1,0:T(8,128)(2,1)S(1)}, u32[]{:S(2)}, u32[]{:S(2)}) collective-permute-start(bf16[6,72,128]{2,1,0:T(8,128)(2,1)S(1)} %fusion), channel_id=1, source_target_pairs={{0,16},{16,0},{1,17},{17,1},{2,18},{18,2},{3,19},{19,3},{4,20},{20... | collective-permute-start | bytes 331784 | tf_op jit(solution)/shard_map/ppermute | solution.py:262
  4.7 0.7 %copy-start.8 = (s32[3]{0:T(128)S(1)}, s32[3]{0:T(128)}, u32[]{:S(2)}) copy-start(s32[3]{0:T(128)} %param.14) | copy-start | bytes 40
  6.7 0.7 %copy-start.4 = (f32[2,256]{1,0:T(2,128)S(1)}, f32[2,256]{1,0:T(2,128)}, u32[]{:S(2)}) copy-start(f32[2,256]{1,0:T(2,128)} %param.19) | copy-start | bytes 6148
  7.4 0.8 %copy-start.1 = (bf16[2,64,2,64]{3,2,1,0:T(2,128)(2,1)S(1)}, bf16[2,64,2,64]{3,2,1,0:T(2,128)(2,1)}, u32[]{:S(2)}) copy-start(bf16[2,64,2,64]{3,2,1,0:T(2,128)(2,1)} %param.17) | copy-start | bytes 98308
  8.3 0.7 %copy-start.3 = (s32[3]{0:T(128)S(1)}, s32[3]{0:T(128)}, u32[]{:S(2)}) copy-start(s32[3]{0:T(128)} %param.15) | copy-start | bytes 40
  13.8 6.4 %collective-permute-start.1 = (bf16[8,72,128]{2,1,0:T(8,128)(2,1)S(1)}, bf16[8,72,128]{2,1,0:T(8,128)(2,1)S(1)}, u32[]{:S(2)}, u32[]{:S(2)}) collective-permute-start(bf16[8,72,128]{2,1,0:T(8,128)(2,1)S(1)} %broadcast_select_fusion.refs_2_.refs_3_.refs_5_), channel_id=1, source_target_pairs={{0,4},{4,8},{8,12},{12,0},{1,5},{5,9},{9,13},{13,1},{2,6},{6,10},{... | collective-permute-start | bytes 442376 | tf_op jit(solution)/shard_map/ppermute | solution.py:19
  15.1 8.4 %collective-permute-start.2 = (bf16[8,72,128]{2,1,0:T(8,128)(2,1)S(1)}, bf16[8,72,128]{2,1,0:T(8,128)(2,1)S(1)}, u32[]{:S(2)}, u32[]{:S(2)}) collective-permute-start(bf16[8,72,128]{2,1,0:T(8,128)(2,1)S(1)} %broadcast_select_fusion.refs_2_.refs_3_.refs_5_), channel_id=1, source_target_pairs={{0,12},{4,0},{8,4},{12,8},{1,13},{5,1},{9,5},{13,9},{2,14},{6,2},{... | collective-permute-start | bytes 442376 | tf_op jit(solution)/shard_map/ppermute | solution.py:19
  23.5 4.2 %copy-start.5 = (f32[2,64]{1,0:T(2,128)S(1)}, f32[2,64]{1,0:T(2,128)}, u32[]{:S(2)}) copy-start(f32[2,64]{1,0:T(2,128)} %param.21) | copy-start | bytes 1540
  23.5 4.2 %copy-start.2 = (bf16[2,64,256]{2,1,0:T(8,128)(2,1)S(1)}, bf16[2,64,256]{2,1,0:T(8,128)(2,1)}, u32[]{:S(2)}) copy-start(bf16[2,64,256]{2,1,0:T(8,128)(2,1)} %param.20) | copy-start | bytes 196612
  23.5 6.9 %collective-permute-start.4 = (bf16[3,8,72,128]{3,2,1,0:T(8,128)(2,1)S(1)}, bf16[3,8,72,128]{3,2,1,0:T(8,128)(2,1)S(1)}, u32[]{:S(2)}, u32[]{:S(2)}) collective-permute-start(bf16[3,8,72,128]{3,2,1,0:T(8,128)(2,1)S(1)} %pad_maximum_fusion), channel_id=1, source_target_pairs={{0,1},{1,0},{2,3},{3,2},{4,5},{5,4},{6,7},{7,6},{8,9},{9,8},{10,11... | collective-permute-start | bytes 1327112 | tf_op jit(solution)/shard_map/ppermute | solution.py:24
  24.7 11.0 %collective-permute-start.3 = (bf16[3,8,72,128]{3,2,1,0:T(8,128)(2,1)S(1)}, bf16[3,8,72,128]{3,2,1,0:T(8,128)(2,1)S(1)}, u32[]{:S(2)}, u32[]{:S(2)}) collective-permute-start(bf16[3,8,72,128]{3,2,1,0:T(8,128)(2,1)S(1)} %pad_maximum_fusion), channel_id=1, source_target_pairs={{1,2},{2,1},{5,6},{6,5},{9,10},{10,9},{13,14},{14,13},{17,18},{18,... | collective-permute-start | bytes 1327112 | tf_op jit(solution)/shard_map/ppermute | solution.py:29
  41.4 6.2 %collective-permute-start.5 = (bf16[7,64,128]{2,1,0:T(8,128)(2,1)S(1)}, bf16[7,64,128]{2,1,0:T(8,128)(2,1)S(1)}, u32[]{:S(2)}, u32[]{:S(2)}) collective-permute-start(bf16[7,64,128]{2,1,0:T(8,128)(2,1)S(1)} %shard_map.111.refs_4_.refs_6_), channel_id=1, source_target_pairs={{0,4},{4,8},{8,12},{12,0},{1,5},{5,9},{9,13},{13,1},{2,6},{6,10},{... | collective-permute-start | bytes 344072 | tf_op jit(solution)/shard_map/ppermute | solution.py:19
  42.3 5.8 %collective-permute-start.6 = (bf16[7,64,128]{2,1,0:T(8,128)(2,1)S(1)}, bf16[7,64,128]{2,1,0:T(8,128)(2,1)S(1)}, u32[]{:S(2)}, u32[]{:S(2)}) collective-permute-start(bf16[7,64,128]{2,1,0:T(8,128)(2,1)S(1)} %shard_map.111.refs_4_.refs_6_), channel_id=1, source_target_pairs={{0,12},{4,0},{8,4},{12,8},{1,13},{5,1},{9,5},{13,9},{2,14},{6,2},{... | collective-permute-start | bytes 344072 | tf_op jit(solution)/shard_map/ppermute | solution.py:19
  48.1 6.1 %collective-permute-start.8 = (bf16[3,7,64,128]{3,2,1,0:T(8,128)(2,1)S(1)}, bf16[3,7,64,128]{3,2,1,0:T(8,128)(2,1)S(1)}, u32[]{:S(2)}, u32[]{:S(2)}) collective-permute-start(bf16[3,7,64,128]{3,2,1,0:T(8,128)(2,1)S(1)} %pad_maximum_fusion.1), channel_id=1, source_target_pairs={{0,1},{1,0},{2,3},{3,2},{4,5},{5,4},{6,7},{7,6},{8,9},{9,8},{10,11... | collective-permute-start | bytes 1032200 | tf_op jit(solution)/shard_map/ppermute | solution.py:24
  48.2 11.2 %collective-permute-start.7 = (bf16[3,7,64,128]{3,2,1,0:T(8,128)(2,1)S(1)}, bf16[3,7,64,128]{3,2,1,0:T(8,128)(2,1)S(1)}, u32[]{:S(2)}, u32[]{:S(2)}) collective-permute-start(bf16[3,7,64,128]{3,2,1,0:T(8,128)(2,1)S(1)} %pad_maximum_fusion.1), channel_id=1, source_target_pairs={{1,2},{2,1},{5,6},{6,5},{9,10},{10,9},{13,14},{14,13},{17,18},{18,... | collective-permute-start | bytes 1032200 | tf_op jit(solution)/shard_map/ppermute | solution.py:29

commit v2 on v1

v2 whole, which is shorter than its diff:
```python
import math

import jax
import jax.numpy as jnp
from jax import lax
from jax.experimental import pallas as pl
from jax.experimental.pallas import tpu as pltpu
from jax.sharding import PartitionSpec as P

EPSILON = 1e-05
FAR = float(2**20)
LOG2E = math.log2(math.e)
HEAD = 8
TERMS = 48
VMEM_LIMIT = 32 * 2**20

MID_START, MID_STOP, LOW, HIGH, MID_AT, OUT_START, OUT_STOP, CUT, COLUMN = range(9)
STEP_Z, FAR_UP, FAR_DOWN, FAR_Z = 4, 5, 6, 7


def whole():
    return pl.BlockSpec(memory_space=pltpu.VMEM)


def scalars():
    return pl.BlockSpec(memory_space=pltpu.SMEM)


def params():
    return pltpu.CompilerParams(vmem_limit_bytes=VMEM_LIMIT)


def shift(block, axis, by):
    count = lax.axis_size(axis)
    return lax.ppermute(block, axis, [(i, (i + by) % count) for i in range(count)])


def partner(block, axis):
    count = lax.axis_size(axis)
    return lax.ppermute(block, axis, [(i, i ^ 1) for i in range(count)])


def crossing(block, axis):
    count = lax.axis_size(axis)
    return lax.ppermute(block, axis, [(i, ((i + 1) ^ 1) - 1) for i in range(1, count - 1)])


def split3(value):
    first = value.astype(jnp.bfloat16).astype(jnp.float32)
    rest = value - first
    second = rest.astype(jnp.bfloat16).astype(jnp.float32)
    return first, second, rest - second


def pack(features, positions, counts, old_cuts, new_cuts, rates, rows):
    slot_rows, _, _, width, slots = features.shape
    peers = lax.axis_size("gx")
    last_y = lax.axis_size("gy") - 1
    last_z = lax.axis_size("gz") - 1
    total = peers * slot_rows // 2

    def body(feat_ref, pos_ref, count_ref, old_ref, new_ref, rate_ref, where_ref, out_ref, int_ref, flt_ref, sem):
        copy = pltpu.make_async_copy(
            feat_ref.at[0:rows, 0, 0], out_ref.at[:, 0:width, :], sem
        )
        copy.start()
        column, row_y, row_z = where_ref[0], where_ref[1], where_ref[2]
        new_low, new_high = new_ref[column], new_ref[column + 1]
        if peers == 2:
            base, mid_at = 0, column
        else:
            base, mid_at = new_low - 2, 1
        int_ref[MID_START] = jnp.maximum(new_low - 1, 0) - base
        int_ref[MID_STOP] = jnp.minimum(new_high + 1, total) - base
        int_ref[LOW] = jnp.int32(0) - base
        int_ref[HIGH] = jnp.int32(total) - base
        int_ref[MID_AT] = jnp.int32(mid_at)
        int_ref[OUT_START] = new_low - base
        int_ref[OUT_STOP] = new_high - base
        int_ref[CUT] = old_ref[1]
        int_ref[COLUMN] = column
        for k in range(2):
            for m in range(2):
                flt_ref[2 * k + m] = rate_ref[k, m]
        flt_ref[STEP_Z] = jnp.where(row_z % 2 == 1, -1.0, 1.0)
        flt_ref[FAR_UP] = jnp.where(row_y == 0, FAR, 0.0)
        flt_ref[FAR_DOWN] = jnp.where(row_y == last_y, FAR, 0.0)
        flt_ref[FAR_Z] = jnp.where(jnp.logical_or(row_z == 0, row_z == last_z), FAR, 0.0)
        lane = lax.broadcasted_iota(jnp.int32, (1, slots), 1)
        spare = jnp.zeros((HEAD - 4, slots), jnp.float32)
        for row in range(rows):
            place = [pos_ref[d, row : row + 1, :].astype(jnp.float32) for d in range(3)]
            far = jnp.where(lane < count_ref[row], 0.0, FAR)
            block = jnp.concatenate(place + [far, spare], axis=0)
            out_ref[row, width : width + HEAD, :] = block.astype(jnp.bfloat16)
        copy.wait()

    where = jnp.stack([lax.axis_index("gx"), lax.axis_index("gy"), lax.axis_index("gz")])
    return pl.pallas_call(
        body,
        out_shape=(
            jax.ShapeDtypeStruct((rows, width + HEAD, slots), jnp.bfloat16),
            jax.ShapeDtypeStruct((9,), jnp.int32),
            jax.ShapeDtypeStruct((8,), jnp.float32),
        ),
        in_specs=[pl.BlockSpec(memory_space=pl.ANY), whole()] + [scalars()] * 5,
        out_specs=(whole(), scalars(), scalars()),
        scratch_shapes=[pltpu.SemaphoreType.DMA],
        compiler_params=params(),
    )(
        features,
        jnp.transpose(positions[:, 0, 0], (1, 0, 2)),
        counts.reshape(-1),
        old_cuts,
        new_cuts,
        rates,
        where,
    )


def assemble(ints, mine, other, rows):
    def body(int_ref, mine_ref, other_ref, out_ref):
        cut, column = int_ref[CUT], int_ref[COLUMN]
        for row in range(rows):
            owner = jnp.int32(row) >= cut
            place = jnp.where(owner, row - cut, row)
            place = jnp.clip(place, 0, mine_ref.shape[0] - 1)
            is_mine = owner.astype(jnp.int32) == column

            @pl.when(is_mine)
            def _(row=row, place=place):
                out_ref[row] = mine_ref[place]

            @pl.when(jnp.logical_not(is_mine))
            def _(row=row, place=place):
                out_ref[row] = other_ref[place]

    return pl.pallas_call(
        body,
        out_shape=jax.ShapeDtypeStruct((rows,) + mine.shape[1:], mine.dtype),
        in_specs=[scalars(), whole(), whole()],
        out_specs=whole(),
        compiler_params=params(),
    )(ints, mine, other)


def centre_terms(place, along, row8):
    here = place.astype(jnp.float32)
    live = row8 < 3
    at = jnp.where(row8 == 0, here + along, jnp.where(live, here, 0.0))
    n1, n2, n3 = split3(jnp.sum(at * at, axis=0, keepdims=True))
    minus = jnp.where(live, -2.0 * here, 0.0)
    norm = jnp.where(row8 == 4, n1, jnp.where(row8 == 5, n2, jnp.where(row8 == 6, n3, 0.0)))
    turned = jnp.sum(jnp.where(row8 == 0, minus, 0.0), axis=0, keepdims=True)
    lead = jnp.where(row8 == 3, 1.0, jnp.where(row8 == 7, turned, minus + norm))
    other = jnp.where(jnp.logical_or(row8 == 0, row8 == 3), -2.0 * along, minus)
    ones = jnp.where(live, 1.0, 0.0)
    stack = jnp.concatenate([lead, other, ones, ones, ones, jnp.zeros_like(ones)], axis=0)
    return stack.T.astype(jnp.bfloat16)


def near_terms(place, base, along, gone, row8):
    move = jnp.where(row8 == 3, base - gone, jnp.where(row8 == 7, -along, base))
    there = place.astype(jnp.float32) - move
    first = there.astype(jnp.bfloat16).astype(jnp.float32)
    rest = there - first
    second = jnp.where(row8 == 0, there, jnp.where(row8 == 3, along, rest))
    at = jnp.where(row8 == 0, there + along, jnp.where(row8 < 3, there, 0.0))
    q1, q2, q3 = split3(at * at)
    stack = jnp.concatenate([first, second, q1, q2, q3, jnp.zeros_like(q1)], axis=0)
    return stack.astype(jnp.bfloat16)


def gather_bins(rows, scales, near_ref, feats, right_ref, feat_at):
    sums = []
    for row in rows:
        right = right_ref[row]
        items = [(c, dx) for c in range(len(feats)) for dx in range(3)]
        total = None
        for k in range(0, len(items), 2):
            lefts = []
            vals = []
            for c, dx in items[k : k + 2]:
                lefts.append(near_ref[c, row + dx])
                source = jnp.clip(row + dx - 1 - feat_at, 0, feats[c].shape[0] - 1)
                vals.append(feats[c][source, :, :])
            left = lefts[0] if len(lefts) == 1 else jnp.concatenate(lefts, axis=1)
            feat = vals[0] if len(vals) == 1 else jnp.concatenate(vals, axis=1)
            dist = jnp.dot(right, left, preferred_element_type=jnp.float32)
            weight = jnp.concatenate(
                [jnp.exp2(dist * scale).astype(jnp.bfloat16) for scale in scales], axis=0
            )
            part = lax.dot_general(
                feat, weight, (((1,), (1,)), ((), ())), preferred_element_type=jnp.float32
            )
            total = part if total is None else total + part
        sums.append(total)
    return sums


def views(spec, arrays, start, size):
    found = []
    for index, sub, *_ in spec:
        ref = arrays[index] if sub is None else arrays[index].at[sub]
        found.append(ref.at[:, start : start + size, :])
    return found


def gather_call(stage, level, ints, flts, spec, frame, feats, right, near, before, extra, out_rows):
    frame_rows, tall, slots = frame.shape
    features = tall - HEAD
    centre = frame_rows // 2
    make_right = right is None
    make_near = near is None
    inputs = [frame] + list(feats)
    if not make_right:
        inputs.append(right)
    if not make_near:
        inputs.append(near)
    if before is not None:
        inputs.append(before)
    inputs += list(extra)
    outs = []
    wide = 2 * slots
    if stage < 2:
        outs.append(jax.ShapeDtypeStruct((out_rows, features, wide), jnp.float32))
    else:
        outs.append(jax.ShapeDtypeStruct((out_rows, features, slots), jnp.bfloat16))
    if make_right:
        outs.append(jax.ShapeDtypeStruct((frame_rows, slots, TERMS), jnp.bfloat16))
    if make_near:
        outs.append(
            jax.ShapeDtypeStruct((len(spec), frame_rows + 2, TERMS, slots), jnp.bfloat16)
        )
    if stage == 0:
        hid = extra[0].shape[2]
        outs.append(jax.ShapeDtypeStruct((hid, features), jnp.bfloat16))
        outs.append(jax.ShapeDtypeStruct((hid, wide), jnp.float32))
        outs.append(jax.ShapeDtypeStruct((features, wide), jnp.float32))

    def body(*refs):
        refs = list(refs)
        ints, flts = refs.pop(0), refs.pop(0)
        home = refs.pop(0)
        vals = [refs.pop(0) for _ in feats]
        right_ref = None if make_right else refs.pop(0)
        near_ref = None if make_near else refs.pop(0)
        prior = None if before is None else refs.pop(0)
        extras = [refs.pop(0) for _ in extra]
        out_ref = refs.pop(0)
        right_ref = refs.pop(0) if make_right else right_ref
        near_ref = refs.pop(0) if make_near else near_ref
        start, stop = (
            (ints[MID_START], ints[MID_STOP]) if level == 0 else (ints[OUT_START], ints[OUT_STOP])
        )
        out_at = ints[MID_AT] if level == 0 else ints[OUT_START]
        feat_at = jnp.int32(0) if level == 0 else ints[MID_AT]
        row8 = lax.broadcasted_iota(jnp.int32, (HEAD, slots), 0)
        scales = [flts[2 * level + m] * -LOG2E for m in range(2)]

        if make_right:
            for row in range(frame_rows):
                place = home[row, features:tall, :]
                right_ref[row] = centre_terms(place, float(centre - row), row8)
        if make_near:
            edge = jnp.where(row8 == 3, FAR, 0.0)
            edge = jnp.concatenate([edge] + [jnp.zeros_like(edge)] * (TERMS // HEAD - 1), axis=0)
            edge = edge.astype(jnp.bfloat16)
            wheres = views(spec, vals, features, HEAD)
            for c, (_, _, dy, dz, flags) in enumerate(spec):
                near_ref[c, 0] = edge
                near_ref[c, frame_rows + 1] = edge
                gone = jnp.float32(0.0)
                for flag in flags:
                    gone = gone + flts[flag]
                base = jnp.where(row8 == 1, float(dy), 0.0)
                base = jnp.where(row8 == 2, float(dz) * flts[STEP_Z], base)
                base = jnp.where(jnp.logical_and(row8 >= 4, row8 <= 6), -1.0, base)
                for row in range(frame_rows):
                    inside = jnp.logical_and(row >= ints[LOW], row < ints[HIGH])
                    lost = gone + jnp.where(inside, 0.0, FAR)
                    near_ref[c, row + 1] = near_terms(
                        wheres[c][row, :, :], base, float(centre - row), lost, row8
                    )
        heads = views(spec, vals, 0, features)

        if stage == 0:
            up_ref, upb_ref, downb_ref = extras
            wup_ref, wupb_ref, wdownb_ref = refs[:3]
            wup_ref[...] = up_ref[level].astype(jnp.float32).T.astype(jnp.bfloat16)
            lift = jnp.broadcast_to(upb_ref[level : level + 1, :], (slots, upb_ref.shape[1])).T
            wupb_ref[...] = jnp.concatenate([lift, lift], axis=1)
            low = jnp.broadcast_to(downb_ref[level : level + 1, :], (slots, features))
            low = jnp.concatenate([low, low], axis=1).T[0:features, :]
            wdownb_ref[...] = jnp.concatenate([low, low], axis=1)

        def pair(turn):
            first = start + 2 * turn
            return [first, jnp.minimum(first + 1, stop - 1)]

        turns = (stop - start + 1) // 2
        if stage < 2:

            def step(turn, carry):
                rows = pair(turn)
                sums = gather_bins(rows, scales, near_ref, heads, right_ref, feat_at)
                for row, total in zip(rows, sums):
                    if prior is not None:
                        total = total + prior[row - out_at]
                    out_ref[row - out_at] = total
                return carry

            lax.fori_loop(0, turns, step, 0)
            return

        centre_ref, conv_ref, down_ref, wup_ref, wupb_ref, wdownb_ref = extras
        gath_ref = refs[0]

        def finish(rows, slot):
            mixed = jnp.dot(conv_ref[level], gath_ref[slot], preferred_element_type=jnp.float32)
            centred = mixed - jnp.mean(mixed, axis=0, keepdims=True)
            spread = jnp.mean(centred * centred, axis=0, keepdims=True)
            normed = (centred * lax.rsqrt(spread + EPSILON)).astype(jnp.bfloat16)
            hidden = jnp.dot(wup_ref[...], normed, preferred_element_type=jnp.float32)
            half = 0.5 * (hidden + wupb_ref[...])
            hidden = (half + half * jnp.tanh(half)).astype(jnp.bfloat16)
            update = jnp.dot(down_ref[level], hidden, preferred_element_type=jnp.float32)
            update = update + wdownb_ref[...]
            for k, row in enumerate(rows):
                source = jnp.clip(row - feat_at, 0, centre_ref.shape[0] - 1)
                kept = centre_ref[source, 0:features, :].astype(jnp.float32)
                far = home[row, features:tall, :].astype(jnp.float32)[3:4, :]
                result = kept + update[:, k * slots : (k + 1) * slots]
                out_ref[row - out_at] = jnp.where(far == 0.0, result, 0.0).astype(jnp.bfloat16)

        for place in range(out_rows):
            out_ref[place] = jnp.zeros((features, slots), jnp.bfloat16)

        def step(turn, carry):
            rows = pair(turn)
            sums = gather_bins(rows, scales, near_ref, heads, right_ref, feat_at)
            finish(pair(jnp.maximum(turn - 1, 0)), (turn + 1) % 2)
            both = []
            for row, total in zip(rows, sums):
                total = total + prior[row - out_at]
                both.append(jnp.concatenate([total[:, :slots], total[:, slots:]], axis=0))
            gath_ref[turn % 2] = jnp.concatenate(both, axis=1).astype(jnp.bfloat16)
            return carry

        lax.fori_loop(0, turns, step, 0)
        finish(pair(turns - 1), (turns + 1) % 2)

    pairs = out_rows * 3 * len(spec)
    scratch = [pltpu.VMEM((2, 2 * features, wide), jnp.bfloat16)] if stage == 2 else []
    return pl.pallas_call(
        body,
        out_shape=tuple(outs),
        in_specs=[scalars(), scalars()] + [whole()] * len(inputs),
        out_specs=tuple(whole() for _ in outs),
        scratch_shapes=scratch,
        cost_estimate=pl.CostEstimate(
            flops=pairs * 2 * slots * slots * (2 * features + TERMS),
            transcendentals=pairs * 2 * slots * slots,
            bytes_accessed=pairs * 4 * slots * slots,
        ),
        compiler_params=params(),
    )(ints, flts, *inputs)


def local(
    features,
    positions,
    counts,
    old_cuts,
    new_cuts,
    radial_rates,
    conv_weight,
    up_weight,
    up_bias,
    down_weight,
    down_bias,
):
    peers = lax.axis_size("gx")
    slot_rows = features.shape[0]
    total = peers * slot_rows // 2
    most = min(slot_rows, total - 2 * (peers - 1))
    packed, ints, flts = pack(
        features, positions, counts, old_cuts, new_cuts, radial_rates, most
    )

    if peers == 2:
        other = lax.ppermute(packed, "gx", [(0, 1), (1, 0)])
        frame = assemble(ints, packed, other, total)
        mid_rows = total - 1
    else:
        column = lax.axis_index("gx")
        old_low = old_cuts[column]
        old_high = old_cuts[column + 1]
        held = old_high - old_low
        frame_rows = slot_rows + 4
        base = new_cuts[column] - 2
        pieces = [packed]
        starts = [old_low]
        for by, rows in ((1, 3), (2, 1)):
            tail_at = jnp.maximum(held - rows, 0)
            tail = lax.dynamic_slice_in_dim(packed, tail_at, rows, 0)
            pieces.append(shift(tail, "gx", by))
            back = jnp.maximum(column - by, 0)
            starts.append(jnp.maximum(old_cuts[back], old_cuts[back + 1] - rows))
            pieces.append(shift(packed[:rows], "gx", -by))
            starts.append(old_cuts[jnp.minimum(column + by, peers - 1)])
        layer = base + jnp.arange(frame_rows, dtype=jnp.int32)
        before = old_cuts[jnp.maximum(column - 1, 0)]
        after = old_cuts[jnp.minimum(column + 1, peers - 1) + 1]
        at = []
        first = 0
        for piece, begin in zip(pieces, starts):
            at.append(first + layer - begin)
            first += piece.shape[0]
        choice = jnp.where(
            layer >= old_high,
            jnp.where(layer >= after, at[4], at[2]),
            jnp.where(layer >= old_low, at[0], jnp.where(layer >= before, at[1], at[3])),
        )
        frame = jnp.take(jnp.concatenate(pieces, axis=0), jnp.clip(choice, 0, first - 1), axis=0)
        mid_rows = slot_rows + 2

    own = [(0, None, 0, 0, ())]
    sides = [
        (0, None, -1, 0, (FAR_UP,)),
        (1, None, 1, 0, (FAR_DOWN,)),
        (2, 0, 0, 1, ()),
        (2, 1, -1, 1, (FAR_UP,)),
        (2, 2, 1, 1, (FAR_DOWN,)),
    ]
    cross = [
        (0, 0, 0, -1, (FAR_Z,)),
        (0, 1, -1, -1, (FAR_UP, FAR_Z)),
        (0, 2, 1, -1, (FAR_DOWN, FAR_Z)),
    ]
    conv = conv_weight.reshape(conv_weight.shape[:2] + (-1,))
    up_turned = jnp.transpose(up_weight, (0, 2, 1))

    def layer_of(level, block, known, out_rows):
        up = shift(block, "gy", 1)
        down = shift(block, "gy", -1)
        right, near0, near1, near2 = known
        made = gather_call(
            0,
            level,
            ints,
            flts,
            own,
            frame,
            [block],
            right,
            near0,
            None,
            [up_turned, up_bias, down_bias],
            out_rows,
        )
        acc, made = made[0], list(made[1:])
        if level == 0:
            right, near0 = made[:2]
        ready = made[-3:]
        acc, up, down = lax.optimization_barrier((acc, up, down))
        trio = jnp.stack([block, up, down])
        far = crossing(trio, "gz")
        close = partner(trio, "gz")
        made = gather_call(
            1, level, ints, flts, sides, frame, [up, down, close], right, near1, acc, [], out_rows
        )
        acc = made[0]
        if level == 0:
            near1 = made[1]
        made = gather_call(
            2,
            level,
            ints,
            flts,
            cross,
            frame,
            [far],
            right,
            near2,
            acc,
            [block, conv, down_weight] + ready,
            out_rows,
        )
        if level == 0:
            near2 = made[1]
        return made[0], (right, near0, near1, near2)

    mid, known = layer_of(0, frame, (None,) * 4, mid_rows)
    moved, _ = layer_of(1, mid, known, slot_rows)
    return moved[:, None, None]


def solution(mesh):
    placed = (P("gx", "gy", "gz", None, None),) * 2 + (P("gx", "gy", "gz"),) + (P(),) * 8
    return jax.shard_map(
        local,
        mesh=mesh,
        in_specs=placed,
        out_specs=P("gx", "gy", "gz", None, None),
        check_vma=False,
    )
```

time: 64.8 us -> 56.2 us (0.87); the launches traced: 65.3 us -> 55.9 us
  local copies, waits for them, and re-layouts: 8.3 us -> 2.4 us
  other arithmetic: 2.61 us -> 0.17 us
  between operations: 1.62 us -> 0.16 us
  starting transfers between devices: 16.2 us -> 17 us
    ppermute x4, waiting for transfers between devices: 9.53 us -> 5.32 us  [shift(): lax.ppermute(block, axis, [(i, (i + by) % count) for i in range(count)])]
    ppermute x1, waiting for transfers between devices: 0.01 us -> 2.76 us  [local(): other = lax.ppermute(packed, 'gx', [(0, 1), (1, 0)])]
    ppermute x4, starting transfers between devices: 6.76 us -> 4.84 us  [shift(): lax.ppermute(block, axis, [(i, (i + by) % count) for i in range(count)])]
    another operation x3 -> x0, local copies, waits for them, and re-layouts: 1.58 us -> none  [the longest x1 1.4 us: local(): jnp.stack([jnp.maximum(new_low - 1, 0) - base, jnp.minimum(new_high + 1,...]
    ppermute x2, waiting for transfers between devices: 0.01 us -> 1.52 us  [crossing(): lax.ppermute(block, axis, [(i, (i + 1 ^ 1) - 1) for i in range(1, count -...]
    ppermute x2, starting transfers between devices: 1.19 us -> 2.62 us  [partner(): return lax.ppermute(block, axis, [(i, i ^ 1) for i in range(count)])]
    ppermute x2, starting transfers between devices: 6.1 us -> 7.37 us  [crossing(): lax.ppermute(block, axis, [(i, (i + 1 ^ 1) - 1) for i in range(1, count -...]
    unnamed x20 -> x22, local copies, waits for them, and re-layouts: 3.49 us -> 2.3 us
  transfers between devices with their start and end apart: 9 -> 9, of which waited for: 4 -> 6; matrix products, arithmetic and copies ran while one was open for 7% -> 0% of each run, Pallas kernels for 24% -> 27%
where the time goes in v2:
time: 56.2 us; the launch traced here: 55.9 us
  Pallas kernels  26.6 us (47%)
  starting transfers between devices  17 us (30%)
  waiting for transfers between devices  9.61 us (17%)
  local copies, waits for them, and re-layouts  2.4 us (4%)
    pallas_call x6, Pallas kernels, gather_call(): pl.pallas_call(body, out_shape=tuple(outs), in_specs=[scalars(), scalars(...  24.8 us
    ppermute x2, starting transfers between devices, crossing(): lax.ppermute(block, axis, [(i, (i + 1 ^ 1) - 1) for i in range(1, count -...  7.37 us
    ppermute x4, waiting for transfers between devices, shift(): lax.ppermute(block, axis, [(i, (i + by) % count) for i in range(count)])  5.32 us
    ppermute x4, starting transfers between devices, shift(): lax.ppermute(block, axis, [(i, (i + by) % count) for i in range(count)])  4.84 us
    ppermute x1, waiting for transfers between devices, local(): other = lax.ppermute(packed, 'gx', [(0, 1), (1, 0)])  2.76 us
    ppermute x2, starting transfers between devices, partner(): return lax.ppermute(block, axis, [(i, i ^ 1) for i in range(count)])  2.62 us
    unnamed x22, local copies, waits for them, and re-layouts  2.3 us
    ppermute x1, starting transfers between devices, local(): other = lax.ppermute(packed, 'gx', [(0, 1), (1, 0)])  2.12 us
  transfers between devices with their start and end apart: 9, of which 6 were waited for; matrix products, arithmetic and copies ran while one was open for 0% of the time, Pallas kernels for 27%

profile of v2, /device:TPU:1, one launch (start us, length us, event | category | flops | bytes accessed | tf_op | source)
XLA Modules:
  0.0 55.9 jit_solution(10800399805810180896)
XLA Ops:
  0.0 0.0 copy-start.1
  0.0 0.1 pad_add_fusion.where_ref
  0.1 0.0 copy-start.4
  0.1 0.0 copy-start.5
  0.1 0.0 copy-start.2
  0.1 0.0 copy-start.3
  0.1 0.6 %copy-done.1 = bf16[8,1,1,3,128]{4,0,3,2,1:T(8,128)(2,1)S(1)} copy-done((bf16[8,1,1,3,128]{4,0,3,2,1:T(8,128)(2,1)S(1)}, bf16[8,1,1,3,128]{4,0,3,2,1:T(8,128)(2,1)}, u32[]{:S(2)}) %copy-start.1) | copy-done | bytes 6168
  0.7 0.0 copy-done.4
  0.7 0.0 copy-done.5
  0.8 0.0 copy-done.2
  0.8 0.0 copy-done.3
  0.8 0.9 %copy-done = bf16[8,1,1,64,128]{4,3,2,1,0:T(8,128)(2,1)S(1)} copy-done((bf16[8,1,1,64,128]{4,3,2,1,0:T(8,128)(2,1)S(1)}, bf16[8,1,1,64,128]{4,3,2,1,0:T(8,128)(2,1)}, u32[]{:S(2)}) %copy-start) | copy-done | bytes 131096
  1.7 1.2 %shard_map.109 = (bf16[6,72,128]{2,1,0:T(8,128)(2,1)S(1)}, s32[9]{0:T(128)S(1)}, f32[8]{0:T(128)S(1)}) custom-call(bf16[8,1,1,64,128]{4,3,2,1,0:T(8,128)(2,1)S(1)} %copy-done, bf16[3,8,128]{2,1,0:T(8,128)(2,1)S(1)} %bitcast.23, s32[8]{0:T(128)S(1)} %bitcast.24, s32[3]{0:T(128)S(1)} %copy-done.4, s32[3]{0:T(128)S(1)} %copy-done.5, f32[2,2]{1,0:T(2,128)S(1)} %copy-done.2, ...), custom_call_target="tpu_custom_call" | custom-call | tf_op jit(solution)/shard_map/pallas_call | solution.py:99
  2.9 2.1 %collective-permute-start = (bf16[6,72,128]{2,1,0:T(8,128)(2,1)S(1)}, bf16[6,72,128]{2,1,0:T(8,128)(2,1)S(1)}, u32[]{:S(2)}, u32[]{:S(2)}) collective-permute-start(bf16[6,72,128]{2,1,0:T(8,128)(2,1)S(1)} %get-tuple-element.30.mine_ref), channel_id=1, source_target_pairs={{0,16},{16,0},{1,17},{17,1},{2,18},{18,2},{3,19},{19,3},{4,20},{20... | collective-permute-start | bytes 331784 | tf_op jit(solution)/shard_map/ppermute | solution.py:392
  5.1 2.8 %collective-permute-done.other_ref = bf16[6,72,128]{2,1,0:T(8,128)(2,1)S(1)} collective-permute-done((bf16[6,72,128]{2,1,0:T(8,128)(2,1)S(1)}, bf16[6,72,128]{2,1,0:T(8,128)(2,1)S(1)}, u32[]{:S(2)}, u32[]{:S(2)}) %collective-permute-start) | collective-permute-done | bytes 110624 | tf_op jit(solution)/shard_map/ppermute | solution.py:392
  7.8 0.0 copy-start.6
  7.8 0.6 %shard_map.110.refs_2_.refs_3_.refs_6_ = bf16[8,72,128]{2,1,0:T(8,128)(2,1)S(1)} custom-call(s32[9]{0:T(128)S(1)} %get-tuple-element.28.int_ref.refs_0_, bf16[6,72,128]{2,1,0:T(8,128)(2,1)S(1)} %get-tuple-element.30.mine_ref, bf16[6,72,128]{2,1,0:T(8,128)(2,1)S(1)} %collective-permute-done.other_ref), custom_call_target="tpu_custom_call" | custom-call | tf_op jit(solution)/shard_map/pallas_call | solution.py:138
  8.5 0.0 copy-start.8
  8.5 3.3 %collective-permute-start.2 = (bf16[8,72,128]{2,1,0:T(8,128)(2,1)S(1)}, bf16[8,72,128]{2,1,0:T(8,128)(2,1)S(1)}, u32[]{:S(2)}, u32[]{:S(2)}) collective-permute-start(bf16[8,72,128]{2,1,0:T(8,128)(2,1)S(1)} %shard_map.110.refs_2_.refs_3_.refs_6_), channel_id=1, source_target_pairs={{0,12},{4,0},{8,4},{12,8},{1,13},{5,1},{9,5},{13,9},{2,14},{6,2},{... | collective-permute-start | bytes 442376 | tf_op jit(solution)/shard_map/ppermute | solution.py:35
  11.8 0.0 collective-permute-start.1
  11.8 0.0 copy-done.6
  11.8 0.0 copy-done.8
  11.8 0.7 %copy-done.9 = f32[2,64]{1,0:T(2,128)S(1)} copy-done((f32[2,64]{1,0:T(2,128)S(1)}, f32[2,64]{1,0:T(2,128)}, u32[]{:S(2)}) %copy-start.9) | copy-done | bytes 536
  12.5 2.7 %shard_map.111 = (f32[7,64,256]{2,1,0:T(8,128)S(1)}, bf16[8,128,48]{2,1,0:T(8,128)(2,1)S(1)}, bf16[1,10,48,128]{3,2,1,0:T(8,128)(2,1)S(1)}, bf16[256,64]{1,0:T(8...) custom-call(s32[9]{0:T(128)S(1)} %get-tuple-element.28.int_ref.refs_0_, f32[8]{0:T(128)S(1)} %get-tuple-element.29.refs_1_, ...), custom_call_target="tpu_custom_call" | custom-call | flops 121110528 | bytes 1376256 | tf_op jit(solution)/shard_map/pallas_call | solution.py:355
  15.2 0.0 collective-permute-done.2.refs_4_
  15.2 2.9 %collective-permute-done.1.refs_3_ = bf16[8,72,128]{2,1,0:T(8,128)(2,1)S(1)} collective-permute-done((bf16[8,72,128]{2,1,0:T(8,128)(2,1)S(1)}, bf16[8,72,128]{2,1,0:T(8,128)(2,1)S(1)}, u32[]{:S(2)}, u32[]{:S(2)}) %collective-permute-start.1) | collective-permute-done | bytes 147488 | tf_op jit(solution)/shard_map/ppermute | solution.py:35
  18.1 0.1 pad_maximum_fusion
  18.1 2.5 %collective-permute-start.4 = (bf16[3,8,72,128]{3,2,1,0:T(8,128)(2,1)S(1)}, bf16[3,8,72,128]{3,2,1,0:T(8,128)(2,1)S(1)}, u32[]{:S(2)}, u32[]{:S(2)}) collective-permute-start(bf16[3,8,72,128]{3,2,1,0:T(8,128)(2,1)S(1)} %pad_maximum_fusion), channel_id=1, source_target_pairs={{0,1},{1,0},{2,3},{3,2},{4,5},{5,4},{6,7},{7,6},{8,9},{9,8},{10,11... | collective-permute-start | bytes 1327112 | tf_op jit(solution)/shard_map/ppermute | solution.py:40
  20.7 3.0 %collective-permute-start.3 = (bf16[3,8,72,128]{3,2,1,0:T(8,128)(2,1)S(1)}, bf16[3,8,72,128]{3,2,1,0:T(8,128)(2,1)S(1)}, u32[]{:S(2)}, u32[]{:S(2)}) collective-permute-start(bf16[3,8,72,128]{3,2,1,0:T(8,128)(2,1)S(1)} %pad_maximum_fusion), channel_id=1, source_target_pairs={{1,2},{2,1},{5,6},{6,5},{9,10},{10,9},{13,14},{14,13},{17,18},{18,... | collective-permute-start | bytes 1327112 | tf_op jit(solution)/shard_map/ppermute | solution.py:45
  23.7 0.0 copy-done.10
  23.7 0.1 reshape.7.refs_7_.refs_8_
  23.8 0.0 collective-permute-done.4.refs_5_
  23.8 0.0 copy-start.7
  23.8 5.0 %shard_map.112 = (f32[7,64,256]{2,1,0:T(8,128)S(1)}, bf16[5,10,48,128]{3,2,1,0:T(8,128)(2,1)S(1)}) custom-call(s32[9]{0:T(128)S(1)} %get-tuple-element.28.int_ref.refs_0_, f32[8]{0:T(128)S(1)} %get-tuple-element.29.refs_1_, bf16[8,72,128]{2,1,0:T(8,128)(2,1)S(1)} %shard_map.110.refs_2_.refs_3_.refs_6_, ...), custom_call_target="tpu_custom_call" | custom-call | flops 605552640 | bytes 6881280 | tf_op jit(solution)/shard_map/pallas_call | solution.py:355
  28.8 1.4 %collective-permute-done.3.refs_3_ = bf16[3,8,72,128]{3,2,1,0:T(8,128)(2,1)S(1)} collective-permute-done((bf16[3,8,72,128]{3,2,1,0:T(8,128)(2,1)S(1)}, bf16[3,8,72,128]{3,2,1,0:T(8,128)(2,1)S(1)}, u32[]{:S(2)}, u32[]{:S(2)}) %collective-permute-start.3) | collective-permute-done | bytes 442400 | tf_op jit(solution)/shard_map/ppermute | solution.py:45
  30.3 0.0 copy-done.7
  30.3 4.6 %shard_map.113 = (bf16[7,64,128]{2,1,0:T(8,128)(2,1)S(1)}, bf16[3,10,48,128]{3,2,1,0:T(8,128)(2,1)S(1)}) custom-call(s32[9]{0:T(128)S(1)} %get-tuple-element.28.int_ref.refs_0_, f32[8]{0:T(128)S(1)} %get-tuple-element.29.refs_1_, bf16[8,72,128]{2,1,0:T(8,128)(2,1)S(1)} %shard_map.110.refs_2_.refs_3_.refs_6_, ...), custom_call_target="tpu_custom_call" | custom-call | flops 363331584 | bytes 4128768 | tf_op jit(solution)/shard_map/pallas_call | solution.py:355
  34.9 0.9 %collective-permute-start.6 = (bf16[7,64,128]{2,1,0:T(8,128)(2,1)S(1)}, bf16[7,64,128]{2,1,0:T(8,128)(2,1)S(1)}, u32[]{:S(2)}, u32[]{:S(2)}) collective-permute-start(bf16[7,64,128]{2,1,0:T(8,128)(2,1)S(1)} %get-tuple-element.40.refs_3_.refs_7_), channel_id=1, source_target_pairs={{0,12},{4,0},{8,4},{12,8},{1,13},{5,1},{9,5},{13,9},{2,14},{6,2},{... | collective-permute-start | bytes 344072 | tf_op jit(solution)/shard_map/ppermute | solution.py:35
  35.8 0.6 %collective-permute-start.5 = (bf16[7,64,128]{2,1,0:T(8,128)(2,1)S(1)}, bf16[7,64,128]{2,1,0:T(8,128)(2,1)S(1)}, u32[]{:S(2)}, u32[]{:S(2)}) collective-permute-start(bf16[7,64,128]{2,1,0:T(8,128)(2,1)S(1)} %get-tuple-element.40.refs_3_.refs_7_), channel_id=1, source_target_pairs={{0,4},{4,8},{8,12},{12,0},{1,5},{5,9},{9,13},{13,1},{2,6},{6,10},{... | collective-permute-start | bytes 344072 | tf_op jit(solution)/shard_map/ppermute | solution.py:35
  36.4 2.6 %shard_map.114 = (f32[8,64,256]{2,1,0:T(8,128)S(1)}, bf16[256,64]{1,0:T(8,128)(2,1)S(1)}, f32[256,256]{1,0:T(8,128)S(1)}, f32[64,256]{1,0:T(8,128)S(1)}) custom-call(s32[9]{0:T(128)S(1)} %get-tuple-element.28.int_ref.refs_0_, f32[8]{0:T(128)S(1)} %get-tuple-element.29.refs_1_, bf16[8,72,128]{2,1,0:T(8,128)(2,1)S(1)} %shard_map.110.refs_2_.refs_3_.refs_6_, ...), custom_call_target="tpu_custom_call" | custom-call | flops 138412032 | bytes 1572864 | tf_op jit(solution)/shard_map/pallas_call | solution.py:355
  39.0 0.8 %collective-permute-done.6.refs_4_ = bf16[7,64,128]{2,1,0:T(8,128)(2,1)S(1)} collective-permute-done((bf16[7,64,128]{2,1,0:T(8,128)(2,1)S(1)}, bf16[7,64,128]{2,1,0:T(8,128)(2,1)S(1)}, u32[]{:S(2)}, u32[]{:S(2)}) %collective-permute-start.6) | collective-permute-done | bytes 114720 | tf_op jit(solution)/shard_map/ppermute | solution.py:35
  39.8 1.6 %collective-permute-done.5.refs_3_ = bf16[7,64,128]{2,1,0:T(8,128)(2,1)S(1)} collective-permute-done((bf16[7,64,128]{2,1,0:T(8,128)(2,1)S(1)}, bf16[7,64,128]{2,1,0:T(8,128)(2,1)S(1)}, u32[]{:S(2)}, u32[]{:S(2)}) %collective-permute-start.5) | collective-permute-done | bytes 114720 | tf_op jit(solution)/shard_map/ppermute | solution.py:35
  41.4 0.1 collective-permute-start.8
  41.5 4.4 %collective-permute-start.7 = (bf16[3,7,64,128]{3,2,1,0:T(8,128)(2,1)S(1)}, bf16[3,7,64,128]{3,2,1,0:T(8,128)(2,1)S(1)}, u32[]{:S(2)}, u32[]{:S(2)}) collective-permute-start(bf16[3,7,64,128]{3,2,1,0:T(8,128)(2,1)S(1)} %pad_maximum_fusion.1), channel_id=1, source_target_pairs={{1,2},{2,1},{5,6},{6,5},{9,10},{10,9},{13,14},{14,13},{17,18},{18,... | collective-permute-start | bytes 1032200 | tf_op jit(solution)/shard_map/ppermute | solution.py:45
  45.9 0.0 collective-permute-done.8.refs_5_
  45.9 4.8 %shard_map.115.refs_6_ = f32[8,64,256]{2,1,0:T(8,128)S(1)} custom-call(s32[9]{0:T(128)S(1)} %get-tuple-element.28.int_ref.refs_0_, f32[8]{0:T(128)S(1)} %get-tuple-element.29.refs_1_, bf16[8,72,128]{2,1,0:T(8,128)(2,1)S(1)} %shard_map.110.refs_2_.refs_3_.refs_6_, bf16[7,64,128]{2,1,0:T(8,128)(2,1)S(1)} %collective-permute-done.5.refs_3_, ...), custom_call_target="tpu_custom_call" | custom-call | flops 692060160 | bytes 7864320 | tf_op jit(solution)/shard_map/pallas_call | solution.py:355
  50.7 0.1 collective-permute-done.7.refs_3_
  50.8 5.1 %shard_map.116 = bf16[8,64,128]{2,1,0:T(8,128)(2,1)} custom-call(s32[9]{0:T(128)S(1)} %get-tuple-element.28.int_ref.refs_0_, f32[8]{0:T(128)S(1)} %get-tuple-element.29.refs_1_, bf16[8,72,128]{2,1,0:T(8,128)(2,1)S(1)} %shard_map.110.refs_2_.refs_3_.refs_6_, bf16[3,7,64,128]{3,2,1,0:T(8,128)(2,1)S(1)} %collective-permute-done.7.refs_3_, ...), custom_call_target="tpu_custom_call" | custom-call | flops 415236096 | bytes 4718592 | tf_op jit(solution)/shard_map/pallas_call | solution.py:355
  (4 shorter events, 0.0 us)
Async XLA Ops:
  0.0 0.7 %copy-start.1 = (bf16[8,1,1,3,128]{4,0,3,2,1:T(8,128)(2,1)S(1)}, bf16[8,1,1,3,128]{4,0,3,2,1:T(8,128)(2,1)}, u32[]{:S(2)}) copy-start(bf16[8,1,1,3,128]{4,0,3,2,1:T(8,128)(2,1)} %param.12) | copy-start | bytes 18436
  0.1 0.7 %copy-start.4 = (s32[3]{0:T(128)S(1)}, s32[3]{0:T(128)}, u32[]{:S(2)}) copy-start(s32[3]{0:T(128)} %old_ref.1) | copy-start | bytes 40
  0.1 0.7 %copy-start.5 = (s32[3]{0:T(128)S(1)}, s32[3]{0:T(128)}, u32[]{:S(2)}) copy-start(s32[3]{0:T(128)} %new_ref.1) | copy-start | bytes 40
  0.1 0.7 %copy-start.2 = (f32[2,2]{1,0:T(2,128)S(1)}, f32[2,2]{1,0:T(2,128)}, u32[]{:S(2)}) copy-start(f32[2,2]{1,0:T(2,128)} %rate_ref.1) | copy-start | bytes 52
  0.1 0.7 %copy-start.3 = (s32[8,1,1]{0,2,1:T(1,128)S(1)}, s32[8,1,1]{0,2,1:T(1,128)}, u32[]{:S(2)}) copy-start(s32[8,1,1]{0,2,1:T(1,128)} %param.13) | copy-start | bytes 100
  0.8 0.9 %copy-start = (bf16[8,1,1,64,128]{4,3,2,1,0:T(8,128)(2,1)S(1)}, bf16[8,1,1,64,128]{4,3,2,1,0:T(8,128)(2,1)}, u32[]{:S(2)}) copy-start(bf16[8,1,1,64,128]{4,3,2,1,0:T(8,128)(2,1)} %feat_ref.1) | copy-start | bytes 393220
  2.9 4.9 %collective-permute-start = (bf16[6,72,128]{2,1,0:T(8,128)(2,1)S(1)}, bf16[6,72,128]{2,1,0:T(8,128)(2,1)S(1)}, u32[]{:S(2)}, u32[]{:S(2)}) collective-permute-start(bf16[6,72,128]{2,1,0:T(8,128)(2,1)S(1)} %get-tuple-element.30.mine_ref), channel_id=1, source_target_pairs={{0,16},{16,0},{1,17},{17,1},{2,18},{18,2},{3,19},{19,3},{4,20},{20... | collective-permute-start | bytes 331784 | tf_op jit(solution)/shard_map/ppermute | solution.py:392
  7.8 4.0 %copy-start.6 = (bf16[2,256,64]{1,2,0:T(8,128)(2,1)S(1)}, bf16[2,256,64]{1,2,0:T(8,128)(2,1)}, u32[]{:S(2)}) copy-start(bf16[2,256,64]{1,2,0:T(8,128)(2,1)} %param.18) | copy-start | bytes 196612
  8.5 3.3 %copy-start.8 = (f32[2,256]{1,0:T(2,128)S(1)}, f32[2,256]{1,0:T(2,128)}, u32[]{:S(2)}) copy-start(f32[2,256]{1,0:T(2,128)} %refs_7_.1) | copy-start | bytes 6148
  8.5 6.7 %collective-permute-start.2 = (bf16[8,72,128]{2,1,0:T(8,128)(2,1)S(1)}, bf16[8,72,128]{2,1,0:T(8,128)(2,1)S(1)}, u32[]{:S(2)}, u32[]{:S(2)}) collective-permute-start(bf16[8,72,128]{2,1,0:T(8,128)(2,1)S(1)} %shard_map.110.refs_2_.refs_3_.refs_6_), channel_id=1, source_target_pairs={{0,12},{4,0},{8,4},{12,8},{1,13},{5,1},{9,5},{13,9},{2,14},{6,2},{... | collective-permute-start | bytes 442376 | tf_op jit(solution)/shard_map/ppermute | solution.py:35
  11.8 6.3 %collective-permute-start.1 = (bf16[8,72,128]{2,1,0:T(8,128)(2,1)S(1)}, bf16[8,72,128]{2,1,0:T(8,128)(2,1)S(1)}, u32[]{:S(2)}, u32[]{:S(2)}) collective-permute-start(bf16[8,72,128]{2,1,0:T(8,128)(2,1)S(1)} %shard_map.110.refs_2_.refs_3_.refs_6_), channel_id=1, source_target_pairs={{0,4},{4,8},{8,12},{12,0},{1,5},{5,9},{9,13},{13,1},{2,6},{6,10},{... | collective-permute-start | bytes 442376 | tf_op jit(solution)/shard_map/ppermute | solution.py:35
  11.8 0.7 %copy-start.9 = (f32[2,64]{1,0:T(2,128)S(1)}, f32[2,64]{1,0:T(2,128)}, u32[]{:S(2)}) copy-start(f32[2,64]{1,0:T(2,128)} %refs_8_.3) | copy-start | bytes 1540
  18.1 5.6 %copy-start.10 = (bf16[2,64,2,64]{3,2,1,0:T(2,128)(2,1)S(1)}, bf16[2,64,2,64]{3,2,1,0:T(2,128)(2,1)}, u32[]{:S(2)}) copy-start(bf16[2,64,2,64]{3,2,1,0:T(2,128)(2,1)} %param.17) | copy-start | bytes 98308
  18.1 5.7 %collective-permute-start.4 = (bf16[3,8,72,128]{3,2,1,0:T(8,128)(2,1)S(1)}, bf16[3,8,72,128]{3,2,1,0:T(8,128)(2,1)S(1)}, u32[]{:S(2)}, u32[]{:S(2)}) collective-permute-start(bf16[3,8,72,128]{3,2,1,0:T(8,128)(2,1)S(1)} %pad_maximum_fusion), channel_id=1, source_target_pairs={{0,1},{1,0},{2,3},{3,2},{4,5},{5,4},{6,7},{7,6},{8,9},{9,8},{10,11... | collective-permute-start | bytes 1327112 | tf_op jit(solution)/shard_map/ppermute | solution.py:40
  20.7 9.6 %collective-permute-start.3 = (bf16[3,8,72,128]{3,2,1,0:T(8,128)(2,1)S(1)}, bf16[3,8,72,128]{3,2,1,0:T(8,128)(2,1)S(1)}, u32[]{:S(2)}, u32[]{:S(2)}) collective-permute-start(bf16[3,8,72,128]{3,2,1,0:T(8,128)(2,1)S(1)} %pad_maximum_fusion), channel_id=1, source_target_pairs={{1,2},{2,1},{5,6},{6,5},{9,10},{10,9},{13,14},{14,13},{17,18},{18,... | collective-permute-start | bytes 1327112 | tf_op jit(solution)/shard_map/ppermute | solution.py:45
  23.8 6.5 %copy-start.7 = (bf16[2,64,256]{2,1,0:T(8,128)(2,1)S(1)}, bf16[2,64,256]{2,1,0:T(8,128)(2,1)}, u32[]{:S(2)}) copy-start(bf16[2,64,256]{2,1,0:T(8,128)(2,1)} %refs_9_.1) | copy-start | bytes 196612
  34.9 4.9 %collective-permute-start.6 = (bf16[7,64,128]{2,1,0:T(8,128)(2,1)S(1)}, bf16[7,64,128]{2,1,0:T(8,128)(2,1)S(1)}, u32[]{:S(2)}, u32[]{:S(2)}) collective-permute-start(bf16[7,64,128]{2,1,0:T(8,128)(2,1)S(1)} %get-tuple-element.40.refs_3_.refs_7_), channel_id=1, source_target_pairs={{0,12},{4,0},{8,4},{12,8},{1,13},{5,1},{9,5},{13,9},{2,14},{6,2},{... | collective-permute-start | bytes 344072 | tf_op jit(solution)/shard_map/ppermute | solution.py:35
  35.8 5.5 %collective-permute-start.5 = (bf16[7,64,128]{2,1,0:T(8,128)(2,1)S(1)}, bf16[7,64,128]{2,1,0:T(8,128)(2,1)S(1)}, u32[]{:S(2)}, u32[]{:S(2)}) collective-permute-start(bf16[7,64,128]{2,1,0:T(8,128)(2,1)S(1)} %get-tuple-element.40.refs_3_.refs_7_), channel_id=1, source_target_pairs={{0,4},{4,8},{8,12},{12,0},{1,5},{5,9},{9,13},{13,1},{2,6},{6,10},{... | collective-permute-start | bytes 344072 | tf_op jit(solution)/shard_map/ppermute | solution.py:35
  41.4 4.4 %collective-permute-start.8 = (bf16[3,7,64,128]{3,2,1,0:T(8,128)(2,1)S(1)}, bf16[3,7,64,128]{3,2,1,0:T(8,128)(2,1)S(1)}, u32[]{:S(2)}, u32[]{:S(2)}) collective-permute-start(bf16[3,7,64,128]{3,2,1,0:T(8,128)(2,1)S(1)} %pad_maximum_fusion.1), channel_id=1, source_target_pairs={{0,1},{1,0},{2,3},{3,2},{4,5},{5,4},{6,7},{7,6},{8,9},{9,8},{10,11... | collective-permute-start | bytes 1032200 | tf_op jit(solution)/shard_map/ppermute | solution.py:40
  41.5 9.3 %collective-permute-start.7 = (bf16[3,7,64,128]{3,2,1,0:T(8,128)(2,1)S(1)}, bf16[3,7,64,128]{3,2,1,0:T(8,128)(2,1)S(1)}, u32[]{:S(2)}, u32[]{:S(2)}) collective-permute-start(bf16[3,7,64,128]{3,2,1,0:T(8,128)(2,1)S(1)} %pad_maximum_fusion.1), channel_id=1, source_target_pairs={{1,2},{2,1},{5,6},{6,5},{9,10},{10,9},{13,14},{14,13},{17,18},{18,... | collective-permute-start | bytes 1032200 | tf_op jit(solution)/shard_map/ppermute | solution.py:45
